TPU v7x, 128 devices: a whole 4x4x4 slice. The times are simulated.
128 devices in a mesh: recv: 16 (over y, z), send: 8 (over x, core).
Axes of the slice: x: 4, y: 4, z: 4, core: 2. Of those that a mesh axis runs over, the one named last changes fastest.
Arguments:
- nodes: bfloat16 [8192, 256], P('recv'), may hold values from -24 to 24
- frames: int32 [8192], replicated, may hold values from 0 to 59, never falling along the last dimension, each value on 1 to 512 neighbouring positions
- pairs: int32 [2, 512], P(None, ('recv', 'send')), may hold values from 0 to 63, as said below
- masks: int32 [512, 128], P(('recv', 'send')), may hold values from 0 to 1, as said below
- d_out: bfloat16 [8192, 256], P('recv'), may hold values from -6 to 6
- w_query: bfloat16 [256, 256], replicated, may hold values from -0.375 to 0.375
- w_key: bfloat16 [256, 256], replicated, may hold values from -0.375 to 0.375
- w_value: bfloat16 [256, 256], replicated, may hold values from -0.375 to 0.375
- w_left: bfloat16 [256, 128], replicated, may hold values from -0.375 to 0.375
- w_right: bfloat16 [256, 128], replicated, may hold values from -0.375 to 0.375
- frame_edge: bfloat16 [128], replicated, may hold values from -4 to 4
- w_bias: bfloat16 [8, 128], replicated, may hold values from -0.5 to 0.5
- w_edge_value: bfloat16 [128, 256], replicated, may hold values from -0.5 to 0.5
- w_out: bfloat16 [256, 256], replicated, may hold values from -0.375 to 0.375
Outputs:
- mixed: bfloat16 [8192, 256], P('recv')
- grad_nodes: float32 [8192, 256], P('recv')
- grad_bias: float32 [8, 128], replicated
- grad_edge_value: float32 [128, 256], replicated
Inputs may be any that keep to these rules, and one draw needn't show every extreme that they name: `pairs`: row 0 holds a slot's receiver block, row 1 its sender block; block b belongs to recv index b // 4. The slots of the device at recv index r have receiver blocks r * 4 to r * 4 + 3. The sender blocks of one receiver block are distinct over all its slots and include the block itself, in a slot at send index 0. On each device, the slots whose sender block belongs to another recv index name blocks of distinct recv indices. `masks`: A slot that pairs a block with itself is all ones; other slots may be all zeros. `frames`: frame ids never fall along the residues; every frame holds a residue.
All inputs are finite; a program needn't handle non-finite values.
Results may differ from a plain program's by a relative error of at most 0.039.
Values may be sent and summed in bfloat16 or wider, within the bound.
No kernel may reach another device: no remote copies, remote signals or barrier semaphores. Data moves between devices by JAX's collectives and lax.ppermute only.
A program may use at most 128 MiB of HBM per device.

v0:
```python
import jax
import jax.numpy as jnp
from jax import lax
from jax.sharding import PartitionSpec as P

NEG_LARGE = -1e30


def sent_together(arrays, axis, split_dim, concat_dim, along):
    ends, at = ([], 0)
    for a in arrays[:-1]:
        at += a.shape[along]
        ends.append(at)
    both = jnp.concatenate(arrays, axis=along)
    return tuple(
        jnp.split(
            lax.all_to_all(both, axis, split_axis=split_dim, concat_axis=concat_dim, tiled=True),
            ends,
            axis=along,
        )
    )


def in_one_piece(arrays, axis, dim, along):
    ends, at = ([], 0)
    for a in arrays[:-1]:
        at += a.shape[along]
        ends.append(at)
    both = jnp.concatenate(arrays, axis=along)
    return tuple(jnp.split(lax.all_gather(both, axis, axis=dim, tiled=True), ends, axis=along))


def over_pieces(x, axis):
    return lax.all_gather(x, axis).sum(0)


def sent_to_all(x, axis):
    copies = jnp.broadcast_to(x, (lax.axis_size(axis), *x.shape))
    return lax.all_to_all(copies, axis, split_axis=0, concat_axis=0, tiled=True)


def over_copies(x, axis):
    return sent_to_all(x, axis).sum(axis=0)


def packed_total(arrays, axis):
    ends = [0]
    for a in arrays:
        ends.append(ends[-1] + a.size)
    total = lax.psum(jnp.concatenate([a.ravel() for a in arrays]), axis)
    return tuple((total[b:e].reshape(a.shape) for a, b, e in zip(arrays, ends, ends[1:])))


def highest(grad_rows, weight):
    return jnp.dot(grad_rows, weight.astype(jnp.float32).T, precision=lax.Precision.HIGHEST)


def add_rows(array, start, update):
    current = lax.dynamic_slice_in_dim(array, start, update.shape[0], 0)
    return lax.dynamic_update_slice_in_dim(array, current + update, start, 0)


def combine_stats(first, second):
    first_top, first_total = first
    second_top, second_total = second
    joined = jnp.maximum(first_top, second_top)
    return (
        joined,
        first_total * jnp.exp(first_top - joined) + second_total * jnp.exp(second_top - joined),
    )


def body(
    nodes,
    frames,
    pairs,
    masks,
    d_out,
    w_query,
    w_key,
    w_value,
    w_left,
    w_right,
    frame_edge,
    w_bias,
    w_edge_value,
    w_out,
):
    rows, width = nodes.shape
    block = masks.shape[1]
    nb_local = rows // block
    slot_count = masks.shape[0]
    head_count, edge_width = w_bias.shape
    att_width = w_query.shape[1]
    head_dim = att_width // head_count
    scale = head_dim ** (-0.5)
    my_recv = lax.axis_index("recv")
    n_recv = lax.axis_size("recv")
    base_row = my_recv * rows
    base_block = my_recv * nb_local

    def project(inputs, weight):
        return jnp.dot(inputs, weight, preferred_element_type=jnp.float32).astype(jnp.bfloat16)

    query = project(nodes, w_query)
    left_here = project(nodes, w_left)
    keys_here = project(nodes, w_key)
    values_here = project(nodes, w_value)
    right_here = project(nodes, w_right)
    send_blocks = pairs[1]
    owners = send_blocks // nb_local
    remote = owners != my_recv
    owner_ids = jnp.arange(n_recv, dtype=jnp.int32)
    hits = (owners[None, :] == owner_ids[:, None]) & remote[None, :]
    wanted = jnp.sum(jnp.where(hits, (send_blocks % nb_local)[None, :], 0), axis=1)
    requested = lax.all_to_all(wanted, "recv", split_axis=0, concat_axis=0, tiled=True)
    replies = (
        jnp.take(keys_here.reshape(nb_local, block, att_width), requested, axis=0),
        jnp.take(values_here.reshape(nb_local, block, att_width), requested, axis=0),
        jnp.take(right_here.reshape(nb_local, block, edge_width), requested, axis=0),
    )
    keys_got, values_got, right_got = sent_together(
        (replies[0], replies[1], replies[2]), "recv", 0, 0, 2
    )
    keys_all = jnp.concatenate([keys_here, keys_got.reshape(n_recv * block, att_width)], axis=0)
    values_all = jnp.concatenate(
        [values_here, values_got.reshape(n_recv * block, att_width)], axis=0
    )
    right_all = jnp.concatenate([right_here, right_got.reshape(n_recv * block, edge_width)], axis=0)

    def table_start(sender):
        owner = sender // nb_local
        return jnp.where(
            owner == my_recv, (sender - base_block) * block, (nb_local + owner) * block
        )

    node_count = keys_all.shape[0]
    frames_here = lax.dynamic_slice_in_dim(frames, base_row, rows)
    edge_gain = frame_edge.astype(jnp.float32)

    def rows_of(array, start):
        return lax.dynamic_slice_in_dim(array, start, block, 0)

    def fetch(slot_at):
        local_block = pairs[0, slot_at] - base_block
        recv_start = local_block * block
        send_start = table_start(pairs[1, slot_at])
        frame_start = pairs[1, slot_at] * block
        query_blk = rows_of(query, recv_start).reshape(block, head_count, head_dim)
        keys_blk = rows_of(keys_all, send_start).reshape(block, head_count, head_dim)
        values_blk = rows_of(values_all, send_start).reshape(block, head_count, head_dim)
        same_frame = (
            rows_of(frames_here, recv_start)[:, None] == rows_of(frames, frame_start)[None, :]
        ).astype(jnp.float32)
        pre_act = (
            rows_of(left_here, recv_start).astype(jnp.float32)[:, None, :]
            + rows_of(right_all, send_start).astype(jnp.float32)[None, :, :]
            + same_frame[:, :, None] * edge_gain[None, None, :]
        )
        edge_feat = jax.nn.silu(pre_act).astype(jnp.bfloat16)
        valid = masks[slot_at] > 0
        logits = (
            jnp.einsum("ihd,jhd->hij", query_blk, keys_blk, preferred_element_type=jnp.float32)
            * scale
        )
        logits = logits + jnp.einsum(
            "ije,he->hij", edge_feat, w_bias, preferred_element_type=jnp.float32
        )
        logits = jnp.where(valid[None, None, :], logits, NEG_LARGE)
        return (
            local_block,
            recv_start,
            send_start,
            query_blk,
            keys_blk,
            values_blk,
            pre_act,
            edge_feat,
            valid,
            logits,
        )

    def skip_empty(slot_at, work, carry):
        return lax.cond(jnp.any(masks[slot_at] > 0), work, lambda state: state, carry)

    def stats_step(slot_at, carry):

        def work(state):
            row_top, row_total = state
            (
                local_block,
                recv_start,
                send_start,
                query_blk,
                keys_blk,
                values_blk,
                pre_act,
                edge_feat,
                valid,
                logits,
            ) = fetch(slot_at)
            slot_top = jnp.max(logits, axis=2)
            slot_total = jnp.sum(
                jnp.where(valid[None, None, :], jnp.exp(logits - slot_top[:, :, None]), 0.0), axis=2
            )
            joined_top, joined_total = combine_stats(
                (row_top[local_block], row_total[local_block]), (slot_top, slot_total)
            )
            return (
                row_top.at[local_block].set(joined_top),
                row_total.at[local_block].set(joined_total),
            )

        return skip_empty(slot_at, work, carry)

    start_stats = (
        jnp.full((nb_local, head_count, block), NEG_LARGE, jnp.float32),
        jnp.zeros((nb_local, head_count, block), jnp.float32),
    )
    local_top, local_total = lax.fori_loop(0, slot_count, stats_step, start_stats)
    all_tops, all_totals = in_one_piece((local_top, local_total), "send", 0, 1)
    n_send = lax.axis_size("send")
    all_tops = all_tops.reshape(n_send, nb_local, head_count, block)
    all_totals = all_totals.reshape(n_send, nb_local, head_count, block)
    row_top = jnp.max(all_tops, axis=0)
    row_total = jnp.sum(all_totals * jnp.exp(all_tops - row_top[None]), axis=0)

    def probs_of(logits, valid, local_block):
        return jnp.where(
            valid[None, None, :],
            jnp.exp(logits - row_top[local_block][:, :, None]) / row_total[local_block][:, :, None],
            0.0,
        )

    def sum_step(slot_at, carry):

        def work(state):
            out_acc, ctx_acc = state
            (
                local_block,
                recv_start,
                send_start,
                query_blk,
                keys_blk,
                values_blk,
                pre_act,
                edge_feat,
                valid,
                logits,
            ) = fetch(slot_at)
            weights = probs_of(logits, valid, local_block).astype(jnp.bfloat16)
            part_out = jnp.einsum(
                "hij,jhd->ihd", weights, values_blk, preferred_element_type=jnp.float32
            ).reshape(block, att_width)
            part_ctx = jnp.einsum(
                "hij,ije->ihe", weights, edge_feat, preferred_element_type=jnp.float32
            ).reshape(block, head_count * edge_width)
            return (
                add_rows(out_acc, recv_start, part_out),
                add_rows(ctx_acc, recv_start, part_ctx),
            )

        return skip_empty(slot_at, work, carry)

    start_sums = (
        jnp.zeros((rows, att_width), jnp.float32),
        jnp.zeros((rows, head_count * edge_width), jnp.float32),
    )
    local_out, local_ctx = lax.fori_loop(0, slot_count, sum_step, start_sums)
    edge_value = w_edge_value.reshape(edge_width, head_count, head_dim)
    edge_value_f = edge_value.astype(jnp.float32)
    d_att = jnp.dot(d_out, w_out.T, preferred_element_type=jnp.float32).astype(jnp.bfloat16)
    d_att_heads = d_att.reshape(rows, head_count, head_dim)
    d_ctx = jnp.einsum(
        "ihd,ehd->ihe", d_att_heads, edge_value, preferred_element_type=jnp.float32
    ).astype(jnp.bfloat16)
    d_att_f = d_att_heads.astype(jnp.float32)
    d_ctx_f = d_ctx.astype(jnp.float32)
    count = local_ctx.shape[0]
    att_sum = over_pieces(
        local_out
        + jnp.einsum(
            "ihe,ehd->ihd",
            local_ctx.reshape(count, head_count, edge_width),
            edge_value_f,
            precision=lax.Precision.HIGHEST,
        ).reshape(count, att_width),
        "send",
    )
    delta = over_pieces(
        jnp.sum(d_att_f * local_out.reshape(rows, head_count, head_dim), axis=2)
        + jnp.sum(d_ctx_f * local_ctx.reshape(rows, head_count, edge_width), axis=2),
        "send",
    )
    attended = att_sum.astype(jnp.bfloat16)
    count = local_ctx.shape[0]
    grad_edge_part = jnp.einsum(
        "ihe,ihd->ehd",
        local_ctx.reshape(count, head_count, edge_width),
        d_att_f,
        precision=lax.Precision.HIGHEST,
    ).reshape(edge_width, att_width)
    mixed = (
        nodes.astype(jnp.float32) + jnp.dot(attended, w_out, preferred_element_type=jnp.float32)
    ).astype(jnp.bfloat16)

    def grad_step(slot_at, carry):

        def work(state):
            grad_query, grad_left, grad_keys, grad_values, grad_right, bias_acc = state
            (
                local_block,
                recv_start,
                send_start,
                query_blk,
                keys_blk,
                values_blk,
                pre_act,
                edge_feat,
                valid,
                logits,
            ) = fetch(slot_at)
            probs = probs_of(logits, valid, local_block)
            weights = probs.astype(jnp.bfloat16)
            datt_blk = rows_of(d_att_heads, recv_start)
            dctx_blk = rows_of(d_ctx, recv_start)
            delta_blk = rows_of(delta, recv_start)
            d_prob = jnp.einsum(
                "ihd,jhd->hij", datt_blk, values_blk, preferred_element_type=jnp.float32
            ) + jnp.einsum("ihe,ije->hij", dctx_blk, edge_feat, preferred_element_type=jnp.float32)
            d_logit = jnp.where(
                valid[None, None, :], probs * (d_prob - delta_blk.T[:, :, None]), 0.0
            ).astype(jnp.bfloat16)
            part_query = (
                jnp.einsum("hij,jhd->ihd", d_logit, keys_blk, preferred_element_type=jnp.float32)
                * scale
            ).reshape(block, att_width)
            part_keys = (
                jnp.einsum("hij,ihd->jhd", d_logit, query_blk, preferred_element_type=jnp.float32)
                * scale
            ).reshape(block, att_width)
            part_values = jnp.einsum(
                "hij,ihd->jhd", weights, datt_blk, preferred_element_type=jnp.float32
            ).reshape(block, att_width)
            bias_acc = bias_acc + jnp.einsum(
                "hij,ije->he", d_logit, edge_feat, preferred_element_type=jnp.float32
            )
            d_edge = jnp.einsum(
                "hij,he->ije", d_logit, w_bias, preferred_element_type=jnp.float32
            ) + jnp.einsum("hij,ihe->ije", weights, dctx_blk, preferred_element_type=jnp.float32)
            sigmoid_v = jax.nn.sigmoid(pre_act)
            d_pre = (d_edge * sigmoid_v * (1.0 + pre_act * (1.0 - sigmoid_v))).astype(jnp.bfloat16)
            grad_query = add_rows(grad_query, recv_start, part_query)
            grad_left = add_rows(grad_left, recv_start, jnp.sum(d_pre, axis=1, dtype=jnp.float32))
            grad_keys = add_rows(grad_keys, send_start, part_keys)
            grad_values = add_rows(grad_values, send_start, part_values)
            grad_right = add_rows(grad_right, send_start, jnp.sum(d_pre, axis=0, dtype=jnp.float32))
            return (grad_query, grad_left, grad_keys, grad_values, grad_right, bias_acc)

        return skip_empty(slot_at, work, carry)

    start_grads = (
        jnp.zeros((rows, att_width), jnp.float32),
        jnp.zeros((rows, edge_width), jnp.float32),
        jnp.zeros((node_count, att_width), jnp.float32),
        jnp.zeros((node_count, att_width), jnp.float32),
        jnp.zeros((node_count, edge_width), jnp.float32),
        jnp.zeros((head_count, edge_width), jnp.float32),
    )
    grad_query, grad_left, grad_keys, grad_values, grad_right, bias_part = lax.fori_loop(
        0, slot_count, grad_step, start_grads
    )
    receiver_part = highest(grad_query, w_query) + highest(grad_left, w_left)
    returning = (
        grad_keys[rows:].reshape(n_recv, block, att_width),
        grad_values[rows:].reshape(n_recv, block, att_width),
        grad_right[rows:].reshape(n_recv, block, edge_width),
    )
    keys_back, values_back, right_back = tuple(
        (
            part.astype(jnp.float32)
            for part in sent_together(
                (
                    returning[0].astype(jnp.bfloat16),
                    returning[1].astype(jnp.bfloat16),
                    returning[2].astype(jnp.bfloat16),
                ),
                "recv",
                0,
                0,
                2,
            )
        )
    )
    placing = (requested[:, None] == jnp.arange(nb_local, dtype=jnp.int32)[None, :]).astype(
        jnp.float32
    )

    def settle(own_rows, returned):
        landed = jnp.einsum("rb,rkc->bkc", placing, returned, precision=lax.Precision.HIGHEST)
        return own_rows + landed.reshape(rows, returned.shape[2])

    node_part = (
        receiver_part
        + highest(settle(grad_keys[:rows], keys_back), w_key)
        + highest(settle(grad_values[:rows], values_back), w_value)
        + highest(settle(grad_right[:rows], right_back), w_right)
    )
    grad_nodes = d_out.astype(jnp.float32) + over_copies(node_part, "send")
    grad_bias, grad_edge_value = packed_total((bias_part, grad_edge_part), ("recv", "send"))
    return (mixed, grad_nodes, grad_bias, grad_edge_value)


def solution(mesh):
    in_specs = (
        P("recv", None),
        P(),
        P(None, ("recv", "send")),
        P(("recv", "send"), None),
        P("recv", None),
        P(),
        P(),
        P(),
        P(),
        P(),
        P(),
        P(),
        P(),
        P(),
    )
    out_specs = (P("recv", None), P("recv", None), P(), P())
    return jax.shard_map(body, mesh=mesh, in_specs=in_specs, out_specs=out_specs, check_vma=False)
```

profile of v0, /device:TPU:1, one launch (start us, length us, event | category | flops | bytes accessed | tf_op | source)
XLA Modules:
  0.0 607.0 jit_solution(10483054932055129295)
XLA Ops:
  9.5 8.6 %all-to-all-start = ((s32[16,1,1]{2,1,0:T(1,128)}), s32[16,1,1]{2,1,0:T(1,128)S(1)}, u32[]{:S(2)}, u32[]{:S(2)}) async-start(s32[16,1,1]{2,1,0:T(1,128)} %copy.142), calls=%async_computation | async-start | bytes 16384 | tf_op jit(solution)/shard_map/all_to_all | solution.py:116
  32.5 4.0 all-to-all-start.1
  45.1 22.7 %all-to-all-done.1 = bf16[16,128,640]{2,1,0:T(8,128)(2,1)S(1)} async-done(((bf16[16,128,640]{2,1,0:T(8,128)(2,1)}), bf16[16,128,640]{2,1,0:T(8,128)(2,1)S(1)}, u32[]{:S(2)}, u32[]{:S(2)}) %all-to-all-start.1) | async-done | bytes 2621472 | tf_op jit(solution)/shard_map/all_to_all | solution.py:17
  77.9 18.0 %while.55 = (s32[]{:T(128)}, f32[4,8,128]{2,1,0:T(8,128)S(1)}, f32[4,8,128]{2,1,0:T(8,128)S(1)}, s32[4,128]{1,0:T(4,128)S(1)}, s32[2,4]{1,0:T(2,128)S(1)}, /*ind...) while((s32[]{:T(128)}, f32[4,8,128]{2,1,0:T(8,128)S(1)}, ...), condition=%wide.region_8.10_spmd, body=%wide.region_1.9_spmd.sunk | while | flops 59709880 | bytes 4042427 | solution.py:220
  79.2 12.7 %conditional.6 = ((f32[4,8,128]{2,1,0:T(8,128)S(1)}, f32[4,8,128]{2,1,0:T(8,128)S(1)})) conditional(s32[]{:T(128)} %convert_element_type.217, (f32[4,8,128]{2,1,0:T(8,128)S(1)}, f32[4,8,128]{2,1,0:T(8,128)S(1)}) %tuple.150, (s32[]{:T(128)}, s32[2,4]{1,0:T(2,128)S(1)}, s32[]{:T(128)}, f32[4,8,128]{2,1,0:T(8,128)S(1)}, s32[4,128]{1,0:T(4,128)S(1)}, ...), branch_computations={%region_3.4_spmd, %region_4.8_spmd} | conditional | flops 59709624 | bytes 4041612 | solution.py:184
  87.6 3.1 fusion
  95.9 57.0 %all_gather.13 = f32[32,16,128]{2,1,0:T(8,128)S(1)} all-gather(f32[4,16,128]{2,1,0:T(8,128)S(1)} %pad_maximum_fusion.6), channel_id=1, replica_groups=mesh['recv'=16,'send'=8] {'send'}, dimensions={0}, use_global_device_ids=true | all-gather | bytes 294912 | tf_op jit(solution)/shard_map/all_gather | solution.py:30
  153.3 25.7 %while.56 = (s32[]{:T(128)}, f32[512,256]{0,1:T(8,128)S(1)}, f32[512,1024]{1,0:T(8,128)S(1)}, s32[4,128]{1,0:T(4,128)}, s32[2,4]{1,0:T(2,128)}, /*index=5*/s32[]...) while((s32[]{:T(128)}, f32[512,256]{0,1:T(8,128)S(1)}, ...), condition=%wide.region_15.17_spmd, body=%wide.region_11.16_spmd.sunk | while | flops 118587808 | bytes 5736573 | solution.py:269
  155.3 17.7 %conditional.7 = ((f32[512,256]{0,1:T(8,128)S(1)}, f32[512,1024]{1,0:T(8,128)S(1)})) conditional(s32[]{:T(128)} %convert_element_type.218, (f32[512,256]{0,1:T(8,128)S(1)}, f32[512,1024]{1,0:T(8,128)S(1)}) %tuple.153, (s32[]{:T(128)}, s32[2,4]{1,0:T(2,128)}, s32[]{:T(128)}, f32[512,256]{0,1:T(8,128)S(1)}, s32[]{:T(128)}, ...), branch_computations={%region_13.14_spmd, %region_14.15_spmd} | conditional | flops 118587552 | bytes 5735710 | solution.py:184
  166.3 3.2 fusion.14
  185.6 65.7 %all-gather.1 = f32[4096,8]{0,1:T(8,128)S(1)} all-gather(f32[512,8]{0,1:T(8,128)S(1)} %add.353), channel_id=3, replica_groups=mesh['recv'=16,'send'=8] {'send'}, dimensions={0}, use_global_device_ids=true | all-gather | bytes 147456 | tf_op jit(solution)/shard_map/all_gather | solution.py:34
  251.3 3.0 copy.153
  261.4 40.1 %while.57 = (s32[]{:T(128)}, f32[512,256]{0,1:T(8,128)}, f32[512,128]{1,0:T(8,128)}, f32[2560,256]{0,1:T(8,128)}, f32[2560,256]{0,1:T(8,128)}, /*index=5*/f32[25...) while((s32[]{:T(128)}, f32[512,256]{0,1:T(8,128)}, ...), condition=%wide.region_26.28_spmd, body=%wide.region_20.27_spmd.sunk | while | flops 295404960 | bytes 26599216 | solution.py:370
  262.7 34.9 %conditional.8 = ((f32[512,256]{0,1:T(8,128)}, f32[512,128]{1,0:T(8,128)}, f32[2560,256]{0,1:T(8,128)}, f32[2560,256]{0,1:T(8,128)}, f32[2560,128]{1,0:T(8,128)}, /*index=5*/f32[8,128]{1,0:T(8,128)})) conditional(s32[]{:T(128)} %convert_element_type.219, (f32[512,256]{0,1:T(8,128)}, f32[512,128]{1,0:T(8,128)}, f32[2560,256]{0,1:T(8,128)}, ...), branch_computations={%region_22.23_spmd, %region_23.26_spmd} | conditional | flops 295404704 | bytes 26598210 | solution.py:184
  272.1 4.0 fusion.28
  279.7 3.9 fusion.41
  289.1 6.9 %convert_reduce_fusion = (f32[128,128]{1,0:T(8,128)S(1)}, f32[128,128]{1,0:T(8,128)S(1)}) fusion(f32[128]{0:T(128)S(1)} %get-tuple-element.1128, f32[128,128]{1,0:T(8,128)S(1)} %compare_convert_fusion.2, f32[128,128]{1,0:T(8,128)S(1)} %dynamic-slice_convert_fusion.4, f32[128,128]{1,0:T(8,128)S(1)} %dynamic-slice_convert_fusion.5, ...), kind=kOutput, calls=%fused_computation.65 | convolution fusion | flops 67076096 | bytes 9241092 | tf_op jit(solution)/shard_map/while/body/eval_jaxpr/cond/branch_1_fun/hij,ihe->ije/dot_general | solution.py:350
  302.9 3.3 copy.154
  312.9 3.2 pad_maximum_fusion.1
  316.1 108.0 %all-to-all-start.2 = ((bf16[16,128,640]{2,1,0:T(8,128)(2,1)}), bf16[16,128,640]{2,1,0:T(8,128)(2,1)}, u32[]{:S(2)}, u32[]{:S(2)}) async-start(bf16[16,128,640]{2,1,0:T(8,128)(2,1)} %pad_maximum_fusion.1), calls=%async_computation.2 | async-start | bytes 5242880 | tf_op jit(solution)/shard_map/all_to_all | solution.py:17
  433.1 25.3 %all-to-all-done.2 = bf16[16,128,640]{2,1,0:T(8,128)(2,1)} async-done(((bf16[16,128,640]{2,1,0:T(8,128)(2,1)}), bf16[16,128,640]{2,1,0:T(8,128)(2,1)}, u32[]{:S(2)}, u32[]{:S(2)}) %all-to-all-start.2) | async-done | bytes 2621472 | tf_op jit(solution)/shard_map/all_to_all | solution.py:17
  471.4 8.4 %all-to-all-start.3 = ((f32[8,512,256]{2,1,0:T(8,128)}), f32[8,512,256]{2,1,0:T(8,128)}, u32[]{:S(2)}, u32[]{:S(2)}) async-start(f32[8,512,256]{2,1,0:T(8,128)} %broadcast_in_dim.151), calls=%async_computation.3 | async-start | bytes 8388608 | tf_op jit(solution)/shard_map/all_to_all | solution.py:39
  479.8 105.2 %all-reduce.2.cloned.1.call-done = f32[33792]{0:T(1024)} async-done(((f32[33792]{0:T(1024)}), f32[33792]{0:T(1024)}) %all-reduce.2.cloned.1.call-update) | async-done | bytes 135184 | tf_op jit(solution)/shard_map/psum | solution.py:50
  591.2 6.0 copy.174
  (229 shorter events, 127.5 us)
Async XLA Ops:
  8.0 174.6 %copy-start = (bf16[256,256]{1,0:T(8,128)(2,1)S(1)}, bf16[256,256]{1,0:T(8,128)(2,1)}, u32[]{:S(2)}) copy-start(bf16[256,256]{1,0:T(8,128)(2,1)} %param.45) | copy-start | bytes 393220
  9.5 15.0 %all-to-all-start = ((s32[16,1,1]{2,1,0:T(1,128)}), s32[16,1,1]{2,1,0:T(1,128)S(1)}, u32[]{:S(2)}, u32[]{:S(2)}) async-start(s32[16,1,1]{2,1,0:T(1,128)} %copy.142), calls=%async_computation | async-start | bytes 16384 | tf_op jit(solution)/shard_map/all_to_all | solution.py:116
  19.3 11.4 %copy-start.9 = (bf16[512,128]{1,0:T(8,128)(2,1)}, bf16[512,128]{1,0:T(8,128)(2,1)S(1)}, u32[]{:S(2)}) copy-start(bf16[512,128]{1,0:T(8,128)(2,1)S(1)} %convolution_convert_fusion.6) | copy-start | bytes 393220
  30.7 7.5 %copy-start.31 = (bf16[128]{0:T(256)(128)(2,1)S(1)}, bf16[128]{0:T(256)(128)(2,1)}, u32[]{:S(2)}) copy-start(bf16[128]{0:T(256)(128)(2,1)} %param.42) | copy-start | bytes 772
  30.7 9.6 %copy-start.7 = (bf16[512,256]{1,0:T(8,128)(2,1)S(1)}, bf16[512,256]{1,0:T(8,128)(2,1)}, u32[]{:S(2)}) copy-start(bf16[512,256]{1,0:T(8,128)(2,1)} %param.32) | copy-start | bytes 786436
  32.5 35.3 %all-to-all-start.1 = ((bf16[16,128,640]{2,1,0:T(8,128)(2,1)}), bf16[16,128,640]{2,1,0:T(8,128)(2,1)S(1)}, u32[]{:S(2)}, u32[]{:S(2)}) async-start(bf16[16,128,640]{2,1,0:T(8,128)(2,1)} %pad_maximum_fusion), calls=%async_computation.1 | async-start | bytes 5242880 | tf_op jit(solution)/shard_map/all_to_all | solution.py:17
  42.2 32.0 %copy-start.10 = (bf16[512,128]{1,0:T(8,128)(2,1)S(1)}, bf16[512,128]{1,0:T(8,128)(2,1)}, u32[]{:S(2)}) copy-start(bf16[512,128]{1,0:T(8,128)(2,1)} %copy-done.9) | copy-start | bytes 393220
  45.1 29.9 %copy-start.12 = (bf16[512,256]{0,1:T(8,128)(2,1)S(1)}, bf16[512,256]{0,1:T(8,128)(2,1)}, u32[]{:S(2)}) copy-start(bf16[512,256]{0,1:T(8,128)(2,1)} %copy.144) | copy-start | bytes 786436
  95.9 57.0 %copy-start.28 = (s32[512]{0:T(512)}, s32[512]{0:T(512)S(1)}, u32[]{:S(2)}) copy-start(s32[512]{0:T(512)S(1)} %get-tuple-element.2262) | copy-start | bytes 6148
  95.9 57.1 %copy-start.11 = (bf16[2560,256]{0,1:T(8,128)(2,1)}, bf16[2560,256]{0,1:T(8,128)(2,1)S(1)}, u32[]{:S(2)}) copy-start(bf16[2560,256]{0,1:T(8,128)(2,1)S(1)} %get-tuple-element.2243) | copy-start | bytes 3932164
  180.4 73.8 %copy-start.5 = (f32[512,256]{0,1:T(8,128)}, f32[512,256]{0,1:T(8,128)S(1)}, u32[]{:S(2)}) copy-start(f32[512,256]{0,1:T(8,128)S(1)} %get-tuple-element.1189) | copy-start | bytes 1572868
  182.6 76.9 %copy-start.1 = (f32[512,1024]{0,1:T(8,128)}, f32[512,1024]{0,1:T(8,128)S(1)}, u32[]{:S(2)}) copy-start(f32[512,1024]{0,1:T(8,128)S(1)} %copy.149) | copy-start | bytes 6291460
  254.3 7.1 %copy-start.25 = (bf16[8,128]{1,0:T(8,128)(2,1)S(1)}, bf16[8,128]{1,0:T(8,128)(2,1)}, u32[]{:S(2)}) copy-start(bf16[8,128]{1,0:T(8,128)(2,1)} %get-tuple-element.2260) | copy-start | bytes 6148
  301.5 7.4 %copy-start.4 = (f32[2560,256]{0,1:T(8,128)S(1)}, f32[2560,256]{0,1:T(8,128)}, u32[]{:S(2)}) copy-start(f32[2560,256]{0,1:T(8,128)} %get-tuple-element.1194) | copy-start | bytes 7864324
  312.9 111.3 %copy-start.2 = (f32[512,1024]{0,1:T(8,128)S(1)}, f32[512,1024]{0,1:T(8,128)}, u32[]{:S(2)}) copy-start(f32[512,1024]{0,1:T(8,128)} %copy-done.1) | copy-start | bytes 6291460
  316.1 113.6 %copy-start.15 = (bf16[128,256]{0,1:T(8,128)(2,1)S(1)}, bf16[128,256]{0,1:T(8,128)(2,1)}, u32[]{:S(2)}) copy-start(bf16[128,256]{0,1:T(8,128)(2,1)} %copy.150) | copy-start | bytes 196612
  316.1 114.4 %copy-start.6 = (f32[512,256]{0,1:T(8,128)S(1)}, f32[512,256]{0,1:T(8,128)}, u32[]{:S(2)}) copy-start(f32[512,256]{0,1:T(8,128)} %copy-done.5) | copy-start | bytes 1572868
  316.1 142.3 %all-to-all-start.2 = ((bf16[16,128,640]{2,1,0:T(8,128)(2,1)}), bf16[16,128,640]{2,1,0:T(8,128)(2,1)}, u32[]{:S(2)}, u32[]{:S(2)}) async-start(bf16[16,128,640]{2,1,0:T(8,128)(2,1)} %pad_maximum_fusion.1), calls=%async_computation.2 | async-start | bytes 5242880 | tf_op jit(solution)/shard_map/all_to_all | solution.py:17
  424.1 7.3 %copy-start.16 = (bf16[256,256]{1,0:T(8,128)(2,1)S(1)}, bf16[256,256]{1,0:T(8,128)(2,1)}, u32[]{:S(2)}) copy-start(bf16[256,256]{1,0:T(8,128)(2,1)} %param.37) | copy-start | bytes 393220
  424.1 160.9 %all-reduce.2.cloned.1.call-start = ((), (), s32[]{:S(2)}) async-start(), calls=%async_computation.4 | async-start | bytes 270336 | tf_op jit(solution)/shard_map/psum | solution.py:50
  424.2 35.3 %copy-start.27 = (s32[16]{0:T(128)S(1)}, s32[16]{0:T(128)}, u32[]{:S(2)}) copy-start(s32[16]{0:T(128)} %copy-done.26) | copy-start | bytes 196
  429.6 161.6 %all-gather.4.cloned.1.call-start = ((), (), s32[]{:S(2)}) async-start(), calls=%async_computation.5 | async-start | bytes 4718592 | tf_op jit(solution)/shard_map/all_gather | solution.py:34
  471.3 119.0 %copy-start.13 = (bf16[512,256]{1,0:T(8,128)(2,1)S(1)}, bf16[512,256]{1,0:T(8,128)(2,1)}, u32[]{:S(2)}) copy-start(bf16[512,256]{1,0:T(8,128)(2,1)} %param.36) | copy-start | bytes 786436
  471.4 116.5 %all-to-all-start.3 = ((f32[8,512,256]{2,1,0:T(8,128)}), f32[8,512,256]{2,1,0:T(8,128)}, u32[]{:S(2)}, u32[]{:S(2)}) async-start(f32[8,512,256]{2,1,0:T(8,128)} %broadcast_in_dim.151), calls=%async_computation.3 | async-start | bytes 8388608 | tf_op jit(solution)/shard_map/all_to_all | solution.py:39
  (16 other events, 82.8 us)
Sparse Core Ops, SparseCore 0:
  429.7 155.1 all-reduce.1
Sparse Core Ops, SparseCore 1:
  431.8 32.5 all-gather.3
where the time goes:
time: 618 us; the launch traced here: 607 us
  waiting for transfers between devices  156 us (25%)
  starting transfers between devices  129 us (21%)
  blocking collectives  123 us (20%)
  local copies, waits for them, and re-layouts  68.4 us (11%)
  matrix products  51.6 us (8%)
  other arithmetic  41.1 us (7%)
  loops' own time  21.8 us (4%)
  between operations  16.4 us (3%)
    all_to_all x2, starting transfers between devices, sent_together(): lax.all_to_all(both, axis, split_axis=split_dim, concat_axis=concat_dim,...  112 us
    psum x1, waiting for transfers between devices, packed_total(): total = lax.psum(jnp.concatenate([a.ravel() for a in arrays]), axis)  105 us
    all_gather x1, blocking collectives, over_pieces(): return lax.all_gather(x, axis).sum(0)  65.7 us
    all_gather x1, blocking collectives, in_one_piece(): lax.all_gather(both, axis, axis=dim, tiled=True)  57 us
    all_to_all x2, waiting for transfers between devices, sent_together(): lax.all_to_all(both, axis, split_axis=split_dim, concat_axis=concat_dim,...  48 us
    another operation x12, loops' own time, skip_empty(): lax.cond(jnp.any(masks[slot_at] > 0), work, lambda state: state, carry)  13.8 us
  transfers between devices with their start and end apart: 6, of which 4 were waited for; matrix products, arithmetic and copies ran while one was open for 7% of the time, Pallas kernels for 0%

commit v1 on v0

v1 whole, which is shorter than its diff:
```python
import functools

import jax
import jax.numpy as jnp
from jax import lax
from jax.experimental import pallas as pl
from jax.experimental.pallas import tpu as pltpu
from jax.sharding import PartitionSpec as P

NEG_LARGE = -1e30
GROUP = 8
F32 = jnp.float32
BF16 = jnp.bfloat16
VMEM_LIMIT = 60 * 1024 * 1024

RECV_BLOCK, LOCAL_BLOCK, OWNER, IS_LOCAL, SEND_BLOCK, LIVE = range(6)
TOP, TOTAL, DELTA, BLOCK_ID = range(4)


def dot(a, b):
    return jnp.dot(a, b, preferred_element_type=F32)


def dot_t(a, b):
    return lax.dot_general(a, b, (((1,), (1,)), ((), ())), preferred_element_type=F32)


def head_lanes(head_count, att_width, rows):
    lane = lax.broadcasted_iota(jnp.int32, (rows, att_width), 1)
    return lane // (att_width // head_count)


def only_head(x, head_of_lane, head):
    return jnp.where(head_of_lane == head, x, jnp.zeros_like(x))


def first_kernel(
    table, frames_here,
    own, local, got, d_out, frames_send, mask,
    w_query, w_key, w_value, w_left, w_right, w_edge_value, w_out, edge_gain, w_bias,
    probs_out, pair_out, ctx_out, stats_out, att_out, query_out, keys_out, datt_out, left_out, right_out,
    qk_s, dp_s, pair_s,
):
    slot = pl.program_id(0)
    block, att_width = query_out.shape
    heads, edge_width = w_bias.shape
    scale = (att_width // heads) ** (-0.5)
    live = table[slot, LIVE] > 0
    block_id = jnp.full((heads, block), table[slot, RECV_BLOCK], jnp.int32).astype(F32)
    stats_out[BLOCK_ID] = block_id

    @pl.when(jnp.logical_not(live))
    def _():
        stats_out[TOP] = jnp.full((heads, block), NEG_LARGE, F32)
        stats_out[TOTAL] = jnp.zeros((heads, block), F32)
        stats_out[DELTA] = jnp.zeros((heads, block), F32)
        att_out[...] = jnp.zeros_like(att_out)
        ctx_out[...] = jnp.zeros_like(ctx_out)
        datt_out[...] = jnp.zeros_like(datt_out)

    @pl.when(live)
    def _():
        own_x = own[...]
        send_x = jnp.where(table[slot, IS_LOCAL] > 0, local[...].astype(F32), got[...].astype(F32)).astype(BF16)
        query = dot(own_x, w_query[...]).astype(BF16)
        keys = dot(send_x, w_key[...]).astype(BF16)
        values = dot(send_x, w_value[...]).astype(BF16)
        left = dot(own_x, w_left[...]).astype(BF16).astype(F32) * 0.5
        right = dot(send_x, w_right[...]).astype(BF16).astype(F32) * 0.5
        d_att = dot_t(d_out[...], w_out[...]).astype(BF16)
        query_out[...] = query
        keys_out[...] = keys
        datt_out[...] = d_att
        left_out[...] = left
        right_out[...] = right
        frame_rows = jnp.broadcast_to(frames_send[...].astype(F32), (block, edge_width)).T.astype(jnp.int32)
        right_same = right + edge_gain[...].astype(F32) * 0.5
        head_of_lane = head_lanes(heads, att_width, block)
        bias_row = w_bias[...].astype(F32)
        values_edge = jnp.concatenate([values, w_edge_value[...]], axis=0)
        for h in range(heads):
            qk_s[pl.ds(h, block, stride=heads), :] = dot_t(only_head(query, head_of_lane, h), keys) * scale
            both = dot_t(only_head(d_att, head_of_lane, h), values_edge)
            dp_s[pl.ds(h, block, stride=heads), :] = both[:, :block]
            pair_s[pl.ds(heads + h, block, stride=2 * heads), :] = both[:, block:]
            pair_s[pl.ds(h, block, stride=2 * heads), :] = jnp.broadcast_to(bias_row[h : h + 1], (block, edge_width))
        valid = jnp.broadcast_to(mask[...], (heads, block)) > 0
        lane = lax.broadcasted_iota(jnp.int32, (heads, block), 1)
        first_row = table[slot, RECV_BLOCK] * block

        def group(at, carry):
            tops, totals, deltas = carry
            for pair in range(GROUP // 2):
                edges, pairs_in = [], []
                for k in range(2):
                    i = at * GROUP + 2 * pair + k
                    half = jnp.where(frame_rows == frames_here[first_row + i], right_same, right)
                    half = half + left_out[pl.ds(i, 1), :]
                    edges.append((half * jnp.tanh(half) + half).astype(BF16))
                    row = pl.multiple_of(i * 2 * heads, 2 * heads)
                    pair_row = pair_s[pl.ds(row, 2 * heads), :].astype(BF16)
                    pair_out[pl.ds(row, 2 * heads), :] = pair_row
                    pairs_in.append(pair_row)
                scores = dot_t(jnp.concatenate(pairs_in, axis=0), jnp.concatenate(edges, axis=0))
                soft = []
                for k in range(2):
                    i = at * GROUP + 2 * pair + k
                    row = pl.multiple_of(i * heads, heads)
                    top_at, col = 2 * heads * k, block * k
                    logits = qk_s[pl.ds(row, heads), :] + scores[top_at : top_at + heads, col : col + block]
                    d_prob = dp_s[pl.ds(row, heads), :] + scores[top_at + heads : top_at + 2 * heads, col : col + block]
                    logits = jnp.where(valid, logits, NEG_LARGE)
                    top = jnp.max(logits, axis=1, keepdims=True)
                    probs = jnp.exp(logits - top)
                    total = jnp.sum(probs, axis=1, keepdims=True)
                    probs = probs / total
                    delta = jnp.sum(probs * d_prob, axis=1, keepdims=True)
                    centred = probs * (d_prob - delta)
                    both = jnp.concatenate([probs, centred], axis=0)
                    probs_out[pl.ds(pl.multiple_of(i * 2 * heads, 2 * heads), 2 * heads), :] = both
                    soft.append(both.astype(BF16))
                    here = lane == i
                    tops = jnp.where(here, top, tops)
                    totals = jnp.where(here, total, totals)
                    deltas = jnp.where(here, delta, deltas)
                sums = dot(jnp.concatenate(soft, axis=0), jnp.concatenate(edges, axis=1))
                for k in range(2):
                    i = at * GROUP + 2 * pair + k
                    top_at, col = 2 * heads * k, edge_width * k
                    ctx_out[pl.ds(pl.multiple_of(i * 2 * heads, 2 * heads), 2 * heads), :] = (
                        sums[top_at : top_at + 2 * heads, col : col + edge_width]
                    )
            return tops, totals, deltas

        zero = jnp.zeros((heads, block), F32)
        tops, totals, deltas = lax.fori_loop(0, block // GROUP, group, (zero, zero, zero))
        stats_out[TOP] = tops
        stats_out[TOTAL] = totals
        stats_out[DELTA] = deltas
        att = jnp.zeros((block, att_width), F32)
        for h in range(heads):
            probs_h = probs_out[pl.ds(h, block, stride=2 * heads), :].astype(BF16)
            ctx_h = ctx_out[pl.ds(h, block, stride=2 * heads), :].astype(BF16)
            att += dot(probs_h, only_head(values, head_of_lane, h))
            att += dot(ctx_h, only_head(w_edge_value[...], head_of_lane, h))
        att_out[...] = att


def shares(stats_all, stats_mine):
    count = stats_all.shape[0]
    mine = stats_mine[BLOCK_ID]
    top = jnp.full_like(mine, NEG_LARGE)
    for q in range(count):
        top = jnp.maximum(top, jnp.where(stats_all[q, BLOCK_ID] == mine, stats_all[q, TOP], NEG_LARGE))
    total = jnp.zeros_like(mine)
    delta = jnp.zeros_like(mine)
    for q in range(count):
        part = jnp.where(
            stats_all[q, BLOCK_ID] == mine, stats_all[q, TOTAL] * jnp.exp(stats_all[q, TOP] - top), 0.0
        )
        total += part
        delta += part * stats_all[q, DELTA]
    share = stats_mine[TOTAL] * jnp.exp(stats_mine[TOP] - top) / total
    return share, stats_mine[DELTA] - delta / total


def mid_kernel(
    table, stats_all, stats_mine, ctx, att, d_att,
    share_out, shift_out, message,
    att_s, edge_s, bias_s,
):
    slot = pl.program_id(0)
    block, att_width = att.shape
    heads = stats_mine.shape[1]
    edge_width = ctx.shape[1]

    @pl.when(slot == 0)
    def _():
        att_s[...] = jnp.zeros_like(att_s)
        edge_s[...] = jnp.zeros_like(edge_s)
        bias_s[...] = jnp.zeros_like(bias_s)

    share, shift = shares(stats_all, stats_mine)
    share_out[...] = share
    shift_out[...] = shift

    @pl.when(table[slot, LIVE] > 0)
    def _():
        spread = (
            head_lanes(heads, att_width, heads) == lax.broadcasted_iota(jnp.int32, (heads, att_width), 0)
        ).astype(F32)
        share_rows = lax.dot_general(
            share, spread, (((0,), (0,)), ((), ())), preferred_element_type=F32, precision=lax.Precision.HIGHEST
        )
        first_row = pl.multiple_of(table[slot, RECV_BLOCK] * block, block)
        att_s[pl.ds(first_row, block), :] += att[...] * share_rows
        scaled = (d_att[...].astype(F32) * share_rows).astype(BF16)
        weights = jnp.concatenate([share, share * shift], axis=0).astype(BF16)
        head_of_lane = head_lanes(heads, att_width, block)
        head_of_row = lax.broadcasted_iota(jnp.int32, (heads, edge_width), 0)
        edge = jnp.zeros((edge_width, att_width), F32)
        bias = jnp.zeros((heads, edge_width), F32)
        for h in range(heads):
            ctx_h = ctx[pl.ds(h, block, stride=2 * heads), :]
            moved_h = ctx[pl.ds(heads + h, block, stride=2 * heads), :].astype(BF16)
            edge += dot(ctx_h.T.astype(BF16), only_head(scaled, head_of_lane, h))
            sums = dot(weights, jnp.concatenate([ctx_h.astype(BF16), moved_h], axis=1))
            bias += jnp.where(head_of_row == h, sums[:heads, edge_width:] + sums[heads:, :edge_width], 0.0)
        edge_s[...] += edge
        bias_s[...] += bias

    @pl.when(slot == pl.num_programs(0) - 1)
    def _():
        n_send = message.shape[0]
        rows = att_s.shape[0] // n_send
        edge_rows = edge_width // n_send
        for s in range(n_send):
            message[s, 0:rows, :] = att_s[s * rows : (s + 1) * rows, :].astype(BF16)
            message[s, rows : rows + edge_rows, :] = edge_s[s * edge_rows : (s + 1) * edge_rows, :].astype(BF16)
            message[s, rows + edge_rows :, :] = jnp.concatenate([bias_s[...]] * (att_width // edge_width), axis=1).astype(BF16)


def grad_kernel(
    table, frames_here,
    share_in, shift_in, probs_in, pair_in, query_in, keys_in, datt_in, left_in, right_in, frames_send,
    w_query, w_key, w_value, w_left, w_right, edge_gain,
    recv_out, send_out,
    rows_s, diag_s, d_edge_s, right_s, same_s, frame_s, grad_right_s, grad_left_s,
):
    slot = pl.program_id(0)
    block, att_width = query_in.shape
    heads = share_in.shape[0]
    edge_width = w_left.shape[1]
    scale = (att_width // heads) ** (-0.5)
    live = table[slot, LIVE] > 0
    tiles = block // 8
    both_heads = 2 * heads

    @pl.when(slot == 0)
    def _():
        diag_s[...] = jnp.zeros_like(diag_s)

    @pl.when(jnp.logical_not(live))
    def _():
        recv_out[...] = jnp.zeros_like(recv_out)
        send_out[...] = jnp.zeros_like(send_out)

    @pl.when(live)
    def _():
        share, shift = share_in[...], shift_in[...]
        right_s[...] = right_in[...]
        same_s[...] = right_in[...] + edge_gain[...].astype(F32) * 0.5
        frame_s[...] = jnp.broadcast_to(frames_send[...].astype(F32), (block, edge_width)).T.astype(jnp.int32)
        grad_right_s[...] = jnp.zeros_like(grad_right_s)
        lane = lax.broadcasted_iota(jnp.int32, (heads, block), 1)
        first_row = table[slot, RECV_BLOCK] * block

        def group(at, carry):
            for k in range(GROUP):
                i = at * GROUP + k
                here = lane == i
                factor = jnp.sum(jnp.where(here, share, 0.0), axis=1, keepdims=True)
                moved = jnp.sum(jnp.where(here, shift, 0.0), axis=1, keepdims=True)
                row = pl.multiple_of(i * both_heads, both_heads)
                probs = probs_in[pl.ds(row, heads), :]
                centred = probs_in[pl.ds(row + heads, heads), :]
                rows_s[pl.ds(row, heads), :] = (centred + moved * probs) * factor
                rows_s[pl.ds(row + heads, heads), :] = probs * factor
                diag_s[both_heads * k : both_heads * (k + 1), edge_width * k : edge_width * (k + 1)] = (
                    pair_in[pl.ds(row, both_heads), :]
                )
            first = pl.multiple_of(at * GROUP * both_heads, GROUP * both_heads)
            across = rows_s[pl.ds(first, GROUP * both_heads), :].T.astype(BF16)
            d_edge_s[...] = dot(across, diag_s[...])
            frame_of = [frames_here[first_row + at * GROUP + k] for k in range(GROUP)]
            left_of = [
                jnp.broadcast_to(left_in[pl.ds(at * GROUP + k, 1), :], (8, edge_width)) for k in range(GROUP)
            ]
            left_sums = [jnp.zeros((8, edge_width), F32) for _ in range(GROUP)]
            for tile in range(tiles):
                span = slice(8 * tile, 8 * tile + 8)
                right_t, same_t, frame_t = right_s[span, :], same_s[span, :], frame_s[span, :]
                right_sum = grad_right_s[span, :]
                for k in range(GROUP):
                    half = jnp.where(frame_t == frame_of[k], same_t, right_t) + left_of[k]
                    tanh = jnp.tanh(half)
                    slope = (1.0 + tanh) * (half - half * tanh + 1.0)
                    d_pre = slope * d_edge_s[span, edge_width * k : edge_width * (k + 1)]
                    right_sum = right_sum + d_pre
                    left_sums[k] = left_sums[k] + d_pre
                grad_right_s[span, :] = right_sum
            for k in range(GROUP):
                grad_left_s[pl.ds(at * GROUP + k, 1), :] = jnp.sum(left_sums[k], axis=0, keepdims=True)
            return carry

        lax.fori_loop(0, block // GROUP, group, 0)
        query, keys, d_att = query_in[...], keys_in[...], datt_in[...]
        head_of_lane = head_lanes(heads, att_width, block)
        grad_query = jnp.zeros((block, att_width), F32)
        grad_keys = jnp.zeros((block, att_width), F32)
        grad_values = jnp.zeros((block, att_width), F32)
        for h in range(heads):
            d_logit = rows_s[pl.ds(h, block, stride=both_heads), :]
            weight = rows_s[pl.ds(heads + h, block, stride=both_heads), :]
            grad_query += dot(d_logit.astype(BF16), only_head(keys, head_of_lane, h))
            grad_keys += dot(d_logit.T.astype(BF16), only_head(query, head_of_lane, h))
            grad_values += dot(weight.T.astype(BF16), only_head(d_att, head_of_lane, h))
        recv_out[...] = dot_t((grad_query * scale).astype(BF16), w_query[...]) + dot_t(
            (grad_left_s[...] * 0.5).astype(BF16), w_left[...]
        )
        send_out[...] = (
            dot_t((grad_keys * scale).astype(BF16), w_key[...])
            + dot_t(grad_values.astype(BF16), w_value[...])
            + dot_t((grad_right_s[...] * 0.5).astype(BF16), w_right[...])
        ).astype(BF16)


def pack_kernel(slot_of_owner, send_part, early, nodes_piece, w_out, message, mixed_piece):
    n_recv, _, att_width = message.shape
    block = send_part.shape[1]
    rows = nodes_piece.shape[0]
    total = early[0].astype(F32)
    for s in range(1, early.shape[0]):
        total += early[s].astype(F32)
    attended = total[:rows].astype(BF16)
    mixed_piece[...] = (nodes_piece[...].astype(F32) + dot(attended, w_out[...])).astype(BF16)
    extra = total[rows:].astype(BF16)

    for r in range(n_recv):
        slot = slot_of_owner[r]

        @pl.when(slot >= 0)
        def _():
            message[r, :block, :] = send_part[jnp.maximum(slot, 0)]

        @pl.when(slot < 0)
        def _():
            message[r, :block, :] = jnp.zeros((block, att_width), BF16)

        message[r, block:, :] = extra


def merge_kernel(
    table, requested, back, recv_part, send_part, mixed_piece, message, bias_out, acc_s
):
    n_recv, _, att_width = back.shape
    slots, block, _ = recv_part.shape
    n_send = message.shape[0]
    rows = mixed_piece.shape[0]
    acc_s[...] = jnp.zeros_like(acc_s)
    for p in range(slots):
        at = pl.multiple_of(table[p, RECV_BLOCK] * block, block)
        acc_s[pl.ds(at, block), :] += recv_part[p]

        @pl.when(table[p, IS_LOCAL] > 0)
        def _():
            to = pl.multiple_of(table[p, LOCAL_BLOCK] * block, block)
            acc_s[pl.ds(to, block), :] += send_part[p].astype(F32)

    extra = jnp.zeros((back.shape[1] - block, att_width), F32)
    for r in range(n_recv):
        extra += back[r, block:, :].astype(F32)

        @pl.when(requested[r] > 0)
        def _():
            to = pl.multiple_of((requested[r] - 1) * block, block)
            acc_s[pl.ds(to, block), :] += back[r, :block, :].astype(F32)

    edge_rows = message.shape[1] - 2 * rows
    for s in range(n_send):
        message[s, :rows, :] = acc_s[s * rows : (s + 1) * rows, :].astype(BF16)
        message[s, rows : 2 * rows, :] = mixed_piece[...]
        message[s, 2 * rows :, :] = extra[:edge_rows].astype(BF16)
    bias_out[...] = extra[edge_rows:, : bias_out.shape[1]]


def last_kernel(parts, d_out_piece, grad_piece):
    rows = d_out_piece.shape[0]
    total = d_out_piece[...].astype(F32)
    for s in range(parts.shape[0]):
        total += parts[s, :rows, :].astype(F32)
    out = total.astype(grad_piece.dtype)
    for s in range(grad_piece.shape[0]):
        grad_piece[s] = out


def params():
    return pltpu.CompilerParams(vmem_limit_bytes=VMEM_LIMIT)


def whole(*shape):
    return pl.BlockSpec(shape, lambda *_: (0,) * len(shape))


def body(
    nodes,
    frames,
    pairs,
    masks,
    d_out,
    w_query,
    w_key,
    w_value,
    w_left,
    w_right,
    frame_edge,
    w_bias,
    w_edge_value,
    w_out,
):
    rows, width = nodes.shape
    slots, block = masks.shape
    nb_local = rows // block
    heads, edge_width = w_bias.shape
    att_width = w_query.shape[1]
    my_recv = lax.axis_index("recv")
    my_send = lax.axis_index("send")
    n_recv = lax.axis_size("recv")
    n_send = lax.axis_size("send")
    base_block = my_recv * nb_local
    piece = rows // n_send
    edge_piece = edge_width // n_send

    recv_blocks, send_blocks = pairs[0], pairs[1]
    owners = send_blocks // nb_local
    is_local = owners == my_recv
    live = jnp.any(masks > 0, axis=1)
    hits = (owners[None, :] == jnp.arange(n_recv, dtype=jnp.int32)[:, None]) & ~is_local[None, :]
    wanted = jnp.sum(jnp.where(hits, (send_blocks % nb_local)[None, :] + 1, 0), axis=1)
    slot_of_owner = jnp.sum(jnp.where(hits, jnp.arange(slots, dtype=jnp.int32)[None, :] + 1, 0), axis=1) - 1
    requested = lax.all_to_all(wanted, "recv", split_axis=0, concat_axis=0, tiled=True)
    table = jnp.stack(
        [
            recv_blocks - base_block,
            jnp.where(is_local, send_blocks - base_block, 0),
            jnp.where(is_local, 0, owners),
            is_local.astype(jnp.int32),
            send_blocks,
            live.astype(jnp.int32),
        ],
        axis=1,
    )
    node_blocks = nodes.reshape(nb_local, block, width)
    replies = jnp.take(node_blocks, jnp.maximum(requested - 1, 0), axis=0)
    got = lax.all_to_all(replies, "recv", split_axis=0, concat_axis=0, tiled=True)

    frames_here = lax.dynamic_slice_in_dim(frames, my_recv * rows, rows)
    frame_rows = frames.reshape(frames.shape[0] // block, 1, block)
    gain = frame_edge.reshape(1, edge_width)
    d_out_blocks = d_out.reshape(nb_local, block, width)

    def per_slot(*shape):
        return pl.BlockSpec((None, *shape), lambda p, *_: (p,) + (0,) * len(shape))

    def shape_of(dtype, *shape):
        return jax.ShapeDtypeStruct((slots, *shape), dtype)

    both = 2 * heads
    outs = (
        (F32, block * both, block),
        (BF16, block * both, edge_width),
        (F32, block * both, edge_width),
        (F32, 4, heads, block),
        (F32, block, att_width),
        (BF16, block, att_width),
        (BF16, block, att_width),
        (BF16, block, att_width),
        (F32, block, edge_width),
        (F32, block, edge_width),
    )
    own_spec = pl.BlockSpec((None, block, width), lambda p, t, f: (t[p, RECV_BLOCK], 0, 0))
    frame_spec = pl.BlockSpec((None, 1, block), lambda p, t, f: (t[p, SEND_BLOCK], 0, 0))
    probs, pair_rows, ctx, stats, att, query, keys, d_att, left, right = pl.pallas_call(
        first_kernel,
        out_shape=tuple(shape_of(*o) for o in outs),
        grid_spec=pltpu.PrefetchScalarGridSpec(
            num_scalar_prefetch=2,
            grid=(slots,),
            in_specs=[
                own_spec,
                pl.BlockSpec((None, block, width), lambda p, t, f: (t[p, LOCAL_BLOCK], 0, 0)),
                pl.BlockSpec((None, block, width), lambda p, t, f: (t[p, OWNER], 0, 0)),
                own_spec,
                frame_spec,
                per_slot(1, block),
                whole(width, att_width),
                whole(width, att_width),
                whole(width, att_width),
                whole(width, edge_width),
                whole(width, edge_width),
                whole(edge_width, att_width),
                whole(att_width, width),
                whole(1, edge_width),
                whole(heads, edge_width),
            ],
            out_specs=[per_slot(*o[1:]) for o in outs],
            scratch_shapes=[
                pltpu.VMEM((block * heads, block), F32),
                pltpu.VMEM((block * heads, block), F32),
                pltpu.VMEM((block * both, edge_width), F32),
            ],
        ),
        compiler_params=params(),
        name="first",
    )(
        table, frames_here, node_blocks, node_blocks, got, d_out_blocks, frame_rows,
        masks.reshape(slots, 1, block), w_query, w_key, w_value, w_left, w_right,
        w_edge_value, w_out, gain, w_bias,
    )

    stats_all = lax.all_gather(stats, "send", axis=0, tiled=True)
    early_rows = piece + edge_piece + heads
    share, shift, early_out = pl.pallas_call(
        mid_kernel,
        out_shape=(
            shape_of(F32, heads, block),
            shape_of(F32, heads, block),
            jax.ShapeDtypeStruct((n_send, early_rows, att_width), BF16),
        ),
        grid_spec=pltpu.PrefetchScalarGridSpec(
            num_scalar_prefetch=1,
            grid=(slots,),
            in_specs=[
                whole(slots * n_send, 4, heads, block),
                per_slot(4, heads, block),
                per_slot(block * both, edge_width),
                per_slot(block, att_width),
                per_slot(block, att_width),
            ],
            out_specs=[
                per_slot(heads, block),
                per_slot(heads, block),
                whole(n_send, early_rows, att_width),
            ],
            scratch_shapes=[
                pltpu.VMEM((rows, att_width), F32),
                pltpu.VMEM((edge_width, att_width), F32),
                pltpu.VMEM((heads, edge_width), F32),
            ],
        ),
        compiler_params=params(),
        name="mid",
    )(table, stats_all, stats, ctx, att, d_att)
    early = lax.all_to_all(early_out, "send", split_axis=0, concat_axis=0, tiled=True)

    recv_part, send_part = pl.pallas_call(
        grad_kernel,
        out_shape=(shape_of(F32, block, att_width), shape_of(BF16, block, att_width)),
        grid_spec=pltpu.PrefetchScalarGridSpec(
            num_scalar_prefetch=2,
            grid=(slots,),
            in_specs=[
                per_slot(heads, block),
                per_slot(heads, block),
                per_slot(block * both, block),
                per_slot(block * both, edge_width),
                per_slot(block, att_width),
                per_slot(block, att_width),
                per_slot(block, att_width),
                per_slot(block, edge_width),
                per_slot(block, edge_width),
                frame_spec,
                whole(width, att_width),
                whole(width, att_width),
                whole(width, att_width),
                whole(width, edge_width),
                whole(width, edge_width),
                whole(1, edge_width),
            ],
            out_specs=[per_slot(block, att_width), per_slot(block, att_width)],
            scratch_shapes=[
                pltpu.VMEM((block * both, block), F32),
                pltpu.VMEM((GROUP * both, GROUP * edge_width), BF16),
                pltpu.VMEM((block, GROUP * edge_width), F32),
                pltpu.VMEM((block, edge_width), F32),
                pltpu.VMEM((block, edge_width), F32),
                pltpu.VMEM((block, edge_width), jnp.int32),
                pltpu.VMEM((block, edge_width), F32),
                pltpu.VMEM((block, edge_width), F32),
            ],
        ),
        compiler_params=params(),
        cost_estimate=pl.CostEstimate(flops=40_000_000_000, bytes_accessed=12_000_000, transcendentals=8_000_000),
        name="grad",
    )(
        table, frames_here, share, shift, probs, pair_rows, query, keys, d_att, left, right, frame_rows,
        w_query, w_key, w_value, w_left, w_right, gain,
    )

    nodes_piece = lax.dynamic_slice_in_dim(nodes, my_send * piece, piece)
    d_out_piece = lax.dynamic_slice_in_dim(d_out, my_send * piece, piece)
    smem = pl.BlockSpec(memory_space=pltpu.SMEM)
    vmem = pl.BlockSpec(memory_space=pltpu.VMEM)
    message, mixed_piece = pl.pallas_call(
        pack_kernel,
        out_shape=(
            jax.ShapeDtypeStruct((n_recv, block + edge_piece + heads, att_width), BF16),
            jax.ShapeDtypeStruct((piece, width), BF16),
        ),
        in_specs=[smem, vmem, vmem, vmem, vmem],
        out_specs=(vmem, vmem),
        compiler_params=params(),
        name="pack",
    )(slot_of_owner, send_part, early, nodes_piece, w_out)
    back = lax.all_to_all(message, "recv", split_axis=0, concat_axis=0, tiled=True)
    message, grad_bias = pl.pallas_call(
        merge_kernel,
        out_shape=(
            jax.ShapeDtypeStruct((n_send, 2 * piece + edge_piece, att_width), BF16),
            jax.ShapeDtypeStruct((heads, edge_width), F32),
        ),
        in_specs=[smem, smem, vmem, vmem, vmem, vmem],
        out_specs=(vmem, vmem),
        scratch_shapes=[pltpu.VMEM((rows, att_width), F32)],
        compiler_params=params(),
        name="merge",
    )(table, requested, back, recv_part, send_part, mixed_piece)
    parts = lax.all_to_all(message, "send", split_axis=0, concat_axis=0, tiled=True)
    grad_out = pl.pallas_call(
        last_kernel,
        out_shape=jax.ShapeDtypeStruct((n_send, piece, width), BF16),
        in_specs=[vmem, vmem],
        out_specs=vmem,
        compiler_params=params(),
        name="last",
    )(parts, d_out_piece)
    grad_nodes = lax.all_to_all(grad_out, "send", split_axis=0, concat_axis=0, tiled=True)
    mixed = parts[:, piece : 2 * piece].reshape(rows, width)
    grad_edge_value = parts[:, 2 * piece :].reshape(edge_width, att_width).astype(F32)
    return (mixed, grad_nodes.reshape(rows, width).astype(F32), grad_bias, grad_edge_value)


def solution(mesh):
    in_specs = (
        P("recv", None),
        P(),
        P(None, ("recv", "send")),
        P(("recv", "send"), None),
        P("recv", None),
        P(),
        P(),
        P(),
        P(),
        P(),
        P(),
        P(),
        P(),
        P(),
    )
    out_specs = (P("recv", None), P("recv", None), P(), P())
    return jax.shard_map(body, mesh=mesh, in_specs=in_specs, out_specs=out_specs, check_vma=False)
```

time: 618 us -> 284 us (0.46); the launches traced: 607 us -> 283 us
  Pallas kernels: 0 us -> 136 us
  waiting for transfers between devices: 156 us -> 28.2 us
  starting transfers between devices: 129 us -> 30.6 us
  local copies, waits for them, and re-layouts: 68.4 us -> 12.3 us
  blocking collectives: 123 us -> 68.8 us
  matrix products: 51.6 us -> 0 us
  other arithmetic: 41.1 us -> 6.26 us
  loops' own time: 21.8 us -> 0 us
  between operations: 16.4 us -> 0.75 us
    pallas_call x0 -> x6, Pallas kernels: none -> 136 us  [the longest x1 92 us: body(): pl.pallas_call(first_kernel, out_shape=tuple((shape_of(*o) for o in outs)...]
    psum x1 -> x0, waiting for transfers between devices: 105 us -> none  [packed_total(): total = lax.psum(jnp.concatenate([a.ravel() for a in arrays]), axis)]
    all_to_all x3 -> x4, starting transfers between devices: 120 us -> 22 us  [the longest x1 10.4 us: body(): lax.all_to_all(message, 'send', split_axis=0, concat_axis=0, tiled=True)]
    all_gather x2 -> x1, blocking collectives: 123 us -> 44.9 us  [body(): stats_all = lax.all_gather(stats, 'send', axis=0, tiled=True)]
    dot_general x34 -> x0, matrix products: 51.6 us -> none  [the longest x3 8.78 us: fetch(): jnp.einsum('ije,he->hij', edge_feat, w_bias, preferred_element_type=jnp.f...]
    all_to_all x3 -> x4, waiting for transfers between devices: 48 us -> 22.8 us  [the longest x1 10.8 us: body(): lax.all_to_all(replies, 'recv', split_axis=0, concat_axis=0, tiled=True)]
    all_to_all x0 -> x1, blocking collectives: none -> 23.9 us  [body(): lax.all_to_all(message, 'recv', split_axis=0, concat_axis=0, tiled=True)]
    another operation x15 -> x0, loops' own time: 21.8 us -> none  [the longest x12 13.8 us: skip_empty(): lax.cond(jnp.any(masks[slot_at] > 0), work, lambda state: state, carry)]
  transfers between devices with their start and end apart: 6 -> 5, of which waited for: 4 -> 4; matrix products, arithmetic and copies ran while one was open for 7% -> 3% of each run, Pallas kernels for 0% -> 10%
where the time goes in v1:
time: 284 us; the launch traced here: 283 us
  Pallas kernels  136 us (48%)
  blocking collectives  68.8 us (24%)
  starting transfers between devices  30.6 us (11%)
  waiting for transfers between devices  28.2 us (10%)
  local copies, waits for them, and re-layouts  12.3 us (4%)
  other arithmetic  6.26 us (2%)
    pallas_call x1, Pallas kernels, body(): pl.pallas_call(first_kernel, out_shape=tuple((shape_of(*o) for o in outs)...  92 us
    all_gather x1, blocking collectives, body(): stats_all = lax.all_gather(stats, 'send', axis=0, tiled=True)  44.9 us
    pallas_call x1, Pallas kernels, body(): pl.pallas_call(grad_kernel, out_shape=(shape_of(F32, block, att_width), s...  29.3 us
    all_to_all x1, blocking collectives, body(): lax.all_to_all(message, 'recv', split_axis=0, concat_axis=0, tiled=True)  23.9 us
    all_to_all x1, waiting for transfers between devices, body(): lax.all_to_all(replies, 'recv', split_axis=0, concat_axis=0, tiled=True)  10.8 us
    all_to_all x1, starting transfers between devices, body(): lax.all_to_all(message, 'send', split_axis=0, concat_axis=0, tiled=True)  10.4 us
    all_to_all x1, waiting for transfers between devices, body(): lax.all_to_all(message, 'send', split_axis=0, concat_axis=0, tiled=True)  8.68 us
    all_to_all x1, starting transfers between devices, body(): lax.all_to_all(wanted, 'recv', split_axis=0, concat_axis=0, tiled=True)  8.59 us
  transfers between devices with their start and end apart: 5, of which 4 were waited for; matrix products, arithmetic and copies ran while one was open for 3% of the time, Pallas kernels for 10%

profile of v1, /device:TPU:1, one launch (start us, length us, event | category | flops | bytes accessed | tf_op | source)
XLA Modules:
  0.0 282.7 jit_solution(1015808483616300621)
XLA Ops:
  2.9 8.6 %all-to-all-start = ((s32[16,1,1]{2,1,0:T(1,128)}), s32[16,1,1]{2,1,0:T(1,128)S(1)}, u32[]{:S(2)}, u32[]{:S(2)}) async-start(s32[16,1,1]{2,1,0:T(1,128)} %copy.52), calls=%async_computation | async-start | bytes 16384 | tf_op jit(solution)/shard_map/all_to_all | solution.py:431
  12.5 5.4 %all-to-all-done = s32[16,1,1]{2,1,0:T(1,128)S(1)} async-done(((s32[16,1,1]{2,1,0:T(1,128)}), s32[16,1,1]{2,1,0:T(1,128)S(1)}, u32[]{:S(2)}, u32[]{:S(2)}) %all-to-all-start) | async-done | bytes 96 | tf_op jit(solution)/shard_map/all_to_all | solution.py:431
  18.5 1.6 gather_fusion
  20.1 1.1 broadcast_select_fusion
  21.3 3.7 %all-to-all-start.1 = ((bf16[16,128,256]{2,1,0:T(8,128)(2,1)}), bf16[16,128,256]{2,1,0:T(8,128)(2,1)S(1)}, u32[]{:S(2)}, u32[]{:S(2)}) async-start(bf16[16,128,256]{2,1,0:T(8,128)(2,1)} %broadcast_select_fusion), calls=%async_computation.1 | async-start | bytes 2097152 | tf_op jit(solution)/shard_map/all_to_all | solution.py:445
  25.0 1.3 dynamic_slice.9.frames_here
  27.1 1.4 constant_dynamic-slice_fusion.1.nodes_piece
  29.0 10.8 %all-to-all-done.1.got = bf16[16,128,256]{2,1,0:T(8,128)(2,1)S(1)} async-done(((bf16[16,128,256]{2,1,0:T(8,128)(2,1)}), bf16[16,128,256]{2,1,0:T(8,128)(2,1)S(1)}, u32[]{:S(2)}, u32[]{:S(2)}) %all-to-all-start.1) | async-done | bytes 1048608 | tf_op jit(solution)/shard_map/all_to_all | solution.py:445
  39.8 1.0 copy-done
  40.8 92.0 %first.1 = (f32[4,2048,128]{2,1,0:T(8,128)}, bf16[4,2048,128]{2,1,0:T(8,128)(2,1)}, f32[4,2048,128]{2,1,0:T(8,128)}, f32[4,4,8,128]{3,2,1,0:T(8,128)}, f32[4,128...) custom-call(s32[4,6]{1,0:T(4,128)} %stack.2.table, ...), custom_call_target="tpu_custom_call" | custom-call | tf_op jit(solution)/shard_map/first/pallas_call | solution.py:473
  132.8 44.9 %all_gather.3.stats_all = f32[32,4,8,128]{3,2,1,0:T(8,128)} all-gather(f32[4,4,8,128]{3,2,1,0:T(8,128)} %get-tuple-element.23.stats_mine), channel_id=1, replica_groups=mesh['recv'=16,'send'=8] {'send'}, dimensions={0}, use_global_device_ids=true | all-gather | bytes 589824 | tf_op jit(solution)/shard_map/all_gather | solution.py:511
  177.7 7.5 %mid.1 = (f32[4,8,128]{2,1,0:T(8,128)}, f32[4,8,128]{2,1,0:T(8,128)}, bf16[8,88,256]{2,1,0:T(8,128)(2,1)}) custom-call(s32[4,6]{1,0:T(4,128)} %stack.2.table, f32[32,4,8,128]{3,2,1,0:T(8,128)} %all_gather.3.stats_all, f32[4,4,8,128]{3,2,1,0:T(8,128)} %get-tuple-element.23.stats_mine, f32[4,2048,128]{2,1,0:T(8,128)} %get-tuple-element.24.ctx, ...), custom_call_target="tpu_custom_call" | custom-call | tf_op jit(solution)/shard_map/mid/pallas_call | solution.py:513
  185.2 3.6 %all-to-all-start.2 = ((bf16[8,88,256]{2,1,0:T(8,128)(2,1)}), bf16[8,88,256]{2,1,0:T(8,128)(2,1)S(1)}, u32[]{:S(2)}, u32[]{:S(2)}) async-start(bf16[8,88,256]{2,1,0:T(8,128)(2,1)} %get-tuple-element.36), calls=%async_computation.2 | async-start | bytes 720896 | tf_op jit(solution)/shard_map/all_to_all | solution.py:544
  188.8 29.3 %grad.1 = (f32[4,128,256]{2,1,0:T(8,128)}, bf16[4,128,256]{2,1,0:T(8,128)(2,1)}) custom-call(s32[4,6]{1,0:T(4,128)} %stack.2.table, s32[512]{0:T(512)} %dynamic_slice.9.frames_here, f32[4,8,128]{2,1,0:T(8,128)} %get-tuple-element.27.share_in, f32[4,8,128]{2,1,0:T(8,128)} %get-tuple-element.28.shift_in, f32[4,2048,128]{2,1,0:T(8,128)} %get-tuple-element.29.probs_in, ...), custom_call_target="tpu_custom_call" | custom-call | flops 40000000000 | bytes 12000000 | tf_op jit(solution)/shard_map/grad/pallas_call | solution.py:546
  218.9 2.5 pack.1
  221.4 23.9 %all_to_all.36.back = bf16[16,152,256]{2,1,0:T(8,128)(2,1)} all-to-all(bf16[16,152,256]{2,1,0:T(8,128)(2,1)} %get-tuple-element.37), channel_id=1, replica_groups=mesh['recv'=16,'send'=8] {'recv'}, dimensions={0} | all-to-all | bytes 2490368 | tf_op jit(solution)/shard_map/all_to_all | solution.py:605
  245.3 2.6 merge.1
  247.9 10.4 %all-to-all-start.4 = ((bf16[8,144,256]{2,1,0:T(8,128)(2,1)}), bf16[8,144,256]{2,1,0:T(8,128)(2,1)S(1)}, u32[]{:S(2)}, u32[]{:S(2)}) async-start(bf16[8,144,256]{2,1,0:T(8,128)(2,1)} %get-tuple-element.40), calls=%async_computation.4 | async-start | bytes 1179648 | tf_op jit(solution)/shard_map/all_to_all | solution.py:618
  258.4 1.4 constant_dynamic-slice_fusion.d_out_piece
  259.8 8.7 %all-to-all-done.4.parts = bf16[8,144,256]{2,1,0:T(8,128)(2,1)S(1)} async-done(((bf16[8,144,256]{2,1,0:T(8,128)(2,1)}), bf16[8,144,256]{2,1,0:T(8,128)(2,1)S(1)}, u32[]{:S(2)}, u32[]{:S(2)}) %all-to-all-start.4) | async-done | bytes 589856 | tf_op jit(solution)/shard_map/all_to_all | solution.py:618
  269.2 1.8 last.1
  271.1 4.3 %all-to-all-start.5 = ((bf16[8,64,256]{2,1,0:T(8,128)(2,1)}), bf16[8,64,256]{2,1,0:T(8,128)(2,1)S(1)}, u32[]{:S(2)}, u32[]{:S(2)}) async-start(bf16[8,64,256]{2,1,0:T(8,128)(2,1)} %last.1), calls=%async_computation.5 | async-start | bytes 524288 | tf_op jit(solution)/shard_map/all_to_all | solution.py:627
  275.3 1.7 slice.18
  278.5 3.3 %all-to-all-done.5 = bf16[8,64,256]{2,1,0:T(8,128)(2,1)S(1)} async-done(((bf16[8,64,256]{2,1,0:T(8,128)(2,1)}), bf16[8,64,256]{2,1,0:T(8,128)(2,1)S(1)}, u32[]{:S(2)}, u32[]{:S(2)}) %all-to-all-start.5) | async-done | bytes 262176 | tf_op jit(solution)/shard_map/all_to_all | solution.py:627
  (28 shorter events, 9.1 us)
Async XLA Ops:
  2.9 15.0 %all-to-all-start = ((s32[16,1,1]{2,1,0:T(1,128)}), s32[16,1,1]{2,1,0:T(1,128)S(1)}, u32[]{:S(2)}, u32[]{:S(2)}) async-start(s32[16,1,1]{2,1,0:T(1,128)} %copy.52), calls=%async_computation | async-start | bytes 16384 | tf_op jit(solution)/shard_map/all_to_all | solution.py:431
  18.5 2.7 copy-start.3
  21.3 18.6 %all-to-all-start.1 = ((bf16[16,128,256]{2,1,0:T(8,128)(2,1)}), bf16[16,128,256]{2,1,0:T(8,128)(2,1)S(1)}, u32[]{:S(2)}, u32[]{:S(2)}) async-start(bf16[16,128,256]{2,1,0:T(8,128)(2,1)} %broadcast_select_fusion), calls=%async_computation.1 | async-start | bytes 2097152 | tf_op jit(solution)/shard_map/all_to_all | solution.py:445
  39.8 1.0 copy-start
  185.2 32.9 %all-to-all-start.2 = ((bf16[8,88,256]{2,1,0:T(8,128)(2,1)}), bf16[8,88,256]{2,1,0:T(8,128)(2,1)S(1)}, u32[]{:S(2)}, u32[]{:S(2)}) async-start(bf16[8,88,256]{2,1,0:T(8,128)(2,1)} %get-tuple-element.36), calls=%async_computation.2 | async-start | bytes 720896 | tf_op jit(solution)/shard_map/all_to_all | solution.py:544
  218.1 0.7 copy-start.2
  247.9 20.5 %all-to-all-start.4 = ((bf16[8,144,256]{2,1,0:T(8,128)(2,1)}), bf16[8,144,256]{2,1,0:T(8,128)(2,1)S(1)}, u32[]{:S(2)}, u32[]{:S(2)}) async-start(bf16[8,144,256]{2,1,0:T(8,128)(2,1)} %get-tuple-element.40), calls=%async_computation.4 | async-start | bytes 1179648 | tf_op jit(solution)/shard_map/all_to_all | solution.py:618
  268.4 0.8 copy-start.1
  271.1 10.8 %all-to-all-start.5 = ((bf16[8,64,256]{2,1,0:T(8,128)(2,1)}), bf16[8,64,256]{2,1,0:T(8,128)(2,1)S(1)}, u32[]{:S(2)}, u32[]{:S(2)}) async-start(bf16[8,64,256]{2,1,0:T(8,128)(2,1)} %last.1), calls=%async_computation.5 | async-start | bytes 524288 | tf_op jit(solution)/shard_map/all_to_all | solution.py:627

commit v2 on v1

--- a/solution.py
+++ b/solution.py
@@ -39,11 +39,12 @@
     own, local, got, d_out, frames_send, mask,
     w_query, w_key, w_value, w_left, w_right, w_edge_value, w_out, edge_gain, w_bias,
     probs_out, pair_out, ctx_out, stats_out, att_out, query_out, keys_out, datt_out, left_out, right_out,
-    qk_s, dp_s, pair_s,
+    qk_s, dp_s, pair_s, edge_s, score_s,
 ):
     slot = pl.program_id(0)
     block, att_width = query_out.shape
     heads, edge_width = w_bias.shape
+    both_heads = 2 * heads
     scale = (att_width // heads) ** (-0.5)
     live = table[slot, LIVE] > 0
     block_id = jnp.full((heads, block), table[slot, RECV_BLOCK], jnp.int32).astype(F32)
@@ -88,52 +89,74 @@
         lane = lax.broadcasted_iota(jnp.int32, (heads, block), 1)
         first_row = table[slot, RECV_BLOCK] * block
 
-        def group(at, carry):
+        groups = block // GROUP
+
+        def edge_stage(at):
+            for k in range(GROUP):
+                i = at * GROUP + k
+                half = jnp.where(frame_rows == frames_here[first_row + i], right_same, right)
+                half = half + left_out[pl.ds(i, 1), :]
+                edge_s[pl.ds(pl.multiple_of(i * block, block), block), :] = (half * jnp.tanh(half) + half).astype(BF16)
+
+        def score_stage(at):
+            for pair in range(GROUP // 2):
+                i = at * GROUP + 2 * pair
+                rows = pl.ds(pl.multiple_of(i * both_heads, 2 * both_heads), 2 * both_heads)
+                pair_rows = pair_s[rows, :].astype(BF16)
+                pair_out[rows, :] = pair_rows
+                scores = dot_t(pair_rows, edge_s[pl.ds(pl.multiple_of(i * block, 2 * block), 2 * block), :])
+                for k in range(2):
+                    row = pl.multiple_of((i + k) * both_heads, both_heads)
+                    score_s[pl.ds(row, both_heads), :] = scores[
+                        both_heads * k : both_heads * (k + 1), block * k : block * (k + 1)
+                    ]
+
+        def soft_stage(at, carry):
             tops, totals, deltas = carry
+            for k in range(GROUP):
+                i = at * GROUP + k
+                row = pl.multiple_of(i * heads, heads)
+                both_row = pl.multiple_of(i * both_heads, both_heads)
+                logits = qk_s[pl.ds(row, heads), :] + score_s[pl.ds(both_row, heads), :]
+                d_prob = dp_s[pl.ds(row, heads), :] + score_s[pl.ds(both_row + heads, heads), :]
+                logits = jnp.where(valid, logits, NEG_LARGE)
+                top = jnp.max(logits, axis=1, keepdims=True)
+                probs = jnp.exp(logits - top)
+                total = jnp.sum(probs, axis=1, keepdims=True)
+                probs = probs * (1.0 / total)
+                delta = jnp.sum(probs * d_prob, axis=1, keepdims=True)
+                probs_out[pl.ds(both_row, heads), :] = probs
+                probs_out[pl.ds(both_row + heads, heads), :] = probs * (d_prob - delta)
+                here = lane == i
+                tops = jnp.where(here, top, tops)
+                totals = jnp.where(here, total, totals)
+                deltas = jnp.where(here, delta, deltas)
+            return tops, totals, deltas
+
+        def ctx_stage(at):
             for pair in range(GROUP // 2):
-                edges, pairs_in = [], []
+                i = at * GROUP + 2 * pair
+                rows = pl.ds(pl.multiple_of(i * both_heads, 2 * both_heads), 2 * both_heads)
+                edges = edge_s[pl.ds(pl.multiple_of(i * block, 2 * block), 2 * block), :]
+                sums = dot(probs_out[rows, :].astype(BF16), jnp.concatenate([edges[:block], edges[block:]], axis=1))
                 for k in range(2):
-                    i = at * GROUP + 2 * pair + k
-                    half = jnp.where(frame_rows == frames_here[first_row + i], right_same, right)
-                    half = half + left_out[pl.ds(i, 1), :]
-                    edges.append((half * jnp.tanh(half) + half).astype(BF16))
-                    row = pl.multiple_of(i * 2 * heads, 2 * heads)
-                    pair_row = pair_s[pl.ds(row, 2 * heads), :].astype(BF16)
-                    pair_out[pl.ds(row, 2 * heads), :] = pair_row
-                    pairs_in.append(pair_row)
-                scores = dot_t(jnp.concatenate(pairs_in, axis=0), jnp.concatenate(edges, axis=0))
-                soft = []
-                for k in range(2):
-                    i = at * GROUP + 2 * pair + k
-                    row = pl.multiple_of(i * heads, heads)
-                    top_at, col = 2 * heads * k, block * k
-                    logits = qk_s[pl.ds(row, heads), :] + scores[top_at : top_at + heads, col : col + block]
-                    d_prob = dp_s[pl.ds(row, heads), :] + scores[top_at + heads : top_at + 2 * heads, col : col + block]
-                    logits = jnp.where(valid, logits, NEG_LARGE)
-                    top = jnp.max(logits, axis=1, keepdims=True)
-                    probs = jnp.exp(logits - top)
-                    total = jnp.sum(probs, axis=1, keepdims=True)
-                    probs = probs / total
-                    delta = jnp.sum(probs * d_prob, axis=1, keepdims=True)
-                    centred = probs * (d_prob - delta)
-                    both = jnp.concatenate([probs, centred], axis=0)
-                    probs_out[pl.ds(pl.multiple_of(i * 2 * heads, 2 * heads), 2 * heads), :] = both
-                    soft.append(both.astype(BF16))
-                    here = lane == i
-                    tops = jnp.where(here, top, tops)
-                    totals = jnp.where(here, total, totals)
-                    deltas = jnp.where(here, delta, deltas)
-                sums = dot(jnp.concatenate(soft, axis=0), jnp.concatenate(edges, axis=1))
-                for k in range(2):
-                    i = at * GROUP + 2 * pair + k
-                    top_at, col = 2 * heads * k, edge_width * k
-                    ctx_out[pl.ds(pl.multiple_of(i * 2 * heads, 2 * heads), 2 * heads), :] = (
-                        sums[top_at : top_at + 2 * heads, col : col + edge_width]
-                    )
-            return tops, totals, deltas
+                    row = pl.multiple_of((i + k) * both_heads, both_heads)
+                    ctx_out[pl.ds(row, both_heads), :] = sums[
+                        both_heads * k : both_heads * (k + 1), edge_width * k : edge_width * (k + 1)
+                    ]
+
+        def step(at, carry):
+            def clamp(x):
+                return jnp.clip(x, 0, groups - 1)
+
+            ctx_stage(clamp(at - 3))
+            carry = soft_stage(clamp(at - 2), carry)
+            score_stage(clamp(at - 1))
+            edge_stage(clamp(at))
+            return carry
 
         zero = jnp.zeros((heads, block), F32)
-        tops, totals, deltas = lax.fori_loop(0, block // GROUP, group, (zero, zero, zero))
+        tops, totals, deltas = lax.fori_loop(0, groups + 3, step, (zero, zero, zero))
         stats_out[TOP] = tops
         stats_out[TOTAL] = totals
         stats_out[DELTA] = deltas
@@ -498,6 +521,8 @@
                 pltpu.VMEM((block * heads, block), F32),
                 pltpu.VMEM((block * heads, block), F32),
                 pltpu.VMEM((block * both, edge_width), F32),
+                pltpu.VMEM((block * block, edge_width), BF16),
+                pltpu.VMEM((block * both, block), F32),
             ],
         ),
         compiler_params=params(),

time: 284 us -> 202 us (0.71)
  Pallas kernels: 136 us -> 74.9 us
  blocking collectives: 68.8 us -> 52.2 us
  starting transfers between devices: 30.6 us -> 26 us
    pallas_call x1, Pallas kernels: 92 us -> 31.1 us  [body(): pl.pallas_call(first_kernel, out_shape=tuple((shape_of(*o) for o in outs)...]
    all_gather x1, blocking collectives: 44.9 us -> 24.6 us  [body(): stats_all = lax.all_gather(stats, 'send', axis=0, tiled=True)]
    all_to_all x1, starting transfers between devices: 10.4 us -> 5.85 us  [body(): lax.all_to_all(message, 'send', split_axis=0, concat_axis=0, tiled=True)]
    all_to_all x1, blocking collectives: 23.9 us -> 27.6 us  [body(): lax.all_to_all(message, 'recv', split_axis=0, concat_axis=0, tiled=True)]
  transfers between devices with their start and end apart: 5 -> 5, of which waited for: 4 -> 4; matrix products, arithmetic and copies ran while one was open for 3% -> 5% of each run, Pallas kernels for 10% -> 15%
where the time goes in v2:
time: 202 us; the launch traced here: 201 us
  Pallas kernels  74.9 us (37%)
  blocking collectives  52.2 us (26%)
  waiting for transfers between devices  28.2 us (14%)
  starting transfers between devices  26 us (13%)
  local copies, waits for them, and re-layouts  12.3 us (6%)
  other arithmetic  6.26 us (3%)
    pallas_call x1, Pallas kernels, body(): pl.pallas_call(first_kernel, out_shape=tuple((shape_of(*o) for o in outs)...  31.1 us
    pallas_call x1, Pallas kernels, body(): pl.pallas_call(grad_kernel, out_shape=(shape_of(F32, block, att_width), s...  29.3 us
    all_to_all x1, blocking collectives, body(): lax.all_to_all(message, 'recv', split_axis=0, concat_axis=0, tiled=True)  27.6 us
    all_gather x1, blocking collectives, body(): stats_all = lax.all_gather(stats, 'send', axis=0, tiled=True)  24.6 us
    all_to_all x1, waiting for transfers between devices, body(): lax.all_to_all(replies, 'recv', split_axis=0, concat_axis=0, tiled=True)  10.8 us
    all_to_all x1, waiting for transfers between devices, body(): lax.all_to_all(message, 'send', split_axis=0, concat_axis=0, tiled=True)  8.71 us
    all_to_all x1, starting transfers between devices, body(): lax.all_to_all(wanted, 'recv', split_axis=0, concat_axis=0, tiled=True)  8.59 us
    pallas_call x1, Pallas kernels, body(): pl.pallas_call(mid_kernel, out_shape=(shape_of(F32, heads, block), shape_...  7.5 us
  transfers between devices with their start and end apart: 5, of which 4 were waited for; matrix products, arithmetic and copies ran while one was open for 5% of the time, Pallas kernels for 15%

profile of v2, /device:TPU:1, one launch (start us, length us, event | category | flops | bytes accessed | tf_op | source)
XLA Modules:
  0.0 200.6 jit_solution(18205639629831986828)
XLA Ops:
  2.9 8.6 %all-to-all-start = ((s32[16,1,1]{2,1,0:T(1,128)}), s32[16,1,1]{2,1,0:T(1,128)S(1)}, u32[]{:S(2)}, u32[]{:S(2)}) async-start(s32[16,1,1]{2,1,0:T(1,128)} %copy.52), calls=%async_computation | async-start | bytes 16384 | tf_op jit(solution)/shard_map/all_to_all | solution.py:454
  12.5 5.4 %all-to-all-done = s32[16,1,1]{2,1,0:T(1,128)S(1)} async-done(((s32[16,1,1]{2,1,0:T(1,128)}), s32[16,1,1]{2,1,0:T(1,128)S(1)}, u32[]{:S(2)}, u32[]{:S(2)}) %all-to-all-start) | async-done | bytes 96 | tf_op jit(solution)/shard_map/all_to_all | solution.py:454
  18.5 1.6 gather_fusion
  20.1 1.1 broadcast_select_fusion
  21.3 3.7 %all-to-all-start.1 = ((bf16[16,128,256]{2,1,0:T(8,128)(2,1)}), bf16[16,128,256]{2,1,0:T(8,128)(2,1)S(1)}, u32[]{:S(2)}, u32[]{:S(2)}) async-start(bf16[16,128,256]{2,1,0:T(8,128)(2,1)} %broadcast_select_fusion), calls=%async_computation.1 | async-start | bytes 2097152 | tf_op jit(solution)/shard_map/all_to_all | solution.py:468
  25.0 1.3 dynamic_slice.9.frames_here
  27.1 1.4 constant_dynamic-slice_fusion.1.nodes_piece
  29.0 10.8 %all-to-all-done.1.got = bf16[16,128,256]{2,1,0:T(8,128)(2,1)S(1)} async-done(((bf16[16,128,256]{2,1,0:T(8,128)(2,1)}), bf16[16,128,256]{2,1,0:T(8,128)(2,1)S(1)}, u32[]{:S(2)}, u32[]{:S(2)}) %all-to-all-start.1) | async-done | bytes 1048608 | tf_op jit(solution)/shard_map/all_to_all | solution.py:468
  39.8 1.0 copy-done
  40.8 31.1 %first.1 = (f32[4,2048,128]{2,1,0:T(8,128)}, bf16[4,2048,128]{2,1,0:T(8,128)(2,1)}, f32[4,2048,128]{2,1,0:T(8,128)}, f32[4,4,8,128]{3,2,1,0:T(8,128)}, f32[4,128...) custom-call(s32[4,6]{1,0:T(4,128)} %stack.2.table, ...), custom_call_target="tpu_custom_call" | custom-call | tf_op jit(solution)/shard_map/first/pallas_call | solution.py:496
  71.9 24.6 %all_gather.3.stats_all = f32[32,4,8,128]{3,2,1,0:T(8,128)} all-gather(f32[4,4,8,128]{3,2,1,0:T(8,128)} %get-tuple-element.23.stats_mine), channel_id=1, replica_groups=mesh['recv'=16,'send'=8] {'send'}, dimensions={0}, use_global_device_ids=true | all-gather | bytes 589824 | tf_op jit(solution)/shard_map/all_gather | solution.py:536
  96.4 7.5 %mid.1 = (f32[4,8,128]{2,1,0:T(8,128)}, f32[4,8,128]{2,1,0:T(8,128)}, bf16[8,88,256]{2,1,0:T(8,128)(2,1)}) custom-call(s32[4,6]{1,0:T(4,128)} %stack.2.table, f32[32,4,8,128]{3,2,1,0:T(8,128)} %all_gather.3.stats_all, f32[4,4,8,128]{3,2,1,0:T(8,128)} %get-tuple-element.23.stats_mine, f32[4,2048,128]{2,1,0:T(8,128)} %get-tuple-element.24.ctx, ...), custom_call_target="tpu_custom_call" | custom-call | tf_op jit(solution)/shard_map/mid/pallas_call | solution.py:538
  103.9 3.6 %all-to-all-start.2 = ((bf16[8,88,256]{2,1,0:T(8,128)(2,1)}), bf16[8,88,256]{2,1,0:T(8,128)(2,1)S(1)}, u32[]{:S(2)}, u32[]{:S(2)}) async-start(bf16[8,88,256]{2,1,0:T(8,128)(2,1)} %get-tuple-element.36), calls=%async_computation.2 | async-start | bytes 720896 | tf_op jit(solution)/shard_map/all_to_all | solution.py:569
  107.5 29.3 %grad.1 = (f32[4,128,256]{2,1,0:T(8,128)}, bf16[4,128,256]{2,1,0:T(8,128)(2,1)}) custom-call(s32[4,6]{1,0:T(4,128)} %stack.2.table, s32[512]{0:T(512)} %dynamic_slice.9.frames_here, f32[4,8,128]{2,1,0:T(8,128)} %get-tuple-element.27.share_in, f32[4,8,128]{2,1,0:T(8,128)} %get-tuple-element.28.shift_in, f32[4,2048,128]{2,1,0:T(8,128)} %get-tuple-element.29.probs_in, ...), custom_call_target="tpu_custom_call" | custom-call | flops 40000000000 | bytes 12000000 | tf_op jit(solution)/shard_map/grad/pallas_call | solution.py:571
  137.6 2.5 %pack.1 = (bf16[16,152,256]{2,1,0:T(8,128)(2,1)}, bf16[64,256]{1,0:T(8,128)(2,1)}) custom-call(s32[16]{0:T(128)} %broadcast_add_fusion.slot_of_owner, bf16[4,128,256]{2,1,0:T(8,128)(2,1)} %get-tuple-element.35.send_part, bf16[8,88,256]{2,1,0:T(8,128)(2,1)} %copy-done.2, bf16[64,256]{1,0:T(8,128)(2,1)} %constant_dynamic-slice_fusion.1.nodes_piece, ...), custom_call_target="tpu_custom_call" | custom-call | tf_op jit(solution)/shard_map/pack/pallas_call | solution.py:619
  140.2 27.6 %all_to_all.36.back = bf16[16,152,256]{2,1,0:T(8,128)(2,1)} all-to-all(bf16[16,152,256]{2,1,0:T(8,128)(2,1)} %get-tuple-element.37), channel_id=1, replica_groups=mesh['recv'=16,'send'=8] {'recv'}, dimensions={0} | all-to-all | bytes 2490368 | tf_op jit(solution)/shard_map/all_to_all | solution.py:630
  167.8 2.6 %merge.1 = (bf16[8,144,256]{2,1,0:T(8,128)(2,1)}, f32[8,128]{1,0:T(8,128)}) custom-call(s32[4,6]{1,0:T(4,128)} %stack.2.table, s32[16]{0:T(128)} %copy-done.3, bf16[16,152,256]{2,1,0:T(8,128)(2,1)} %all_to_all.36.back, f32[4,128,256]{2,1,0:T(8,128)} %get-tuple-element.38.recv_part, bf16[4,128,256]{2,1,0:T(8,128)(2,1)} %get-tuple-element.35.send_part, ...), custom_call_target="tpu_custom_call" | custom-call | tf_op jit(solution)/shard_map/merge/pallas_call | solution.py:631
  170.4 5.9 %all-to-all-start.4 = ((bf16[8,144,256]{2,1,0:T(8,128)(2,1)}), bf16[8,144,256]{2,1,0:T(8,128)(2,1)S(1)}, u32[]{:S(2)}, u32[]{:S(2)}) async-start(bf16[8,144,256]{2,1,0:T(8,128)(2,1)} %get-tuple-element.40), calls=%async_computation.4 | async-start | bytes 1179648 | tf_op jit(solution)/shard_map/all_to_all | solution.py:643
  176.3 1.4 constant_dynamic-slice_fusion.d_out_piece
  177.6 8.7 %all-to-all-done.4.parts = bf16[8,144,256]{2,1,0:T(8,128)(2,1)S(1)} async-done(((bf16[8,144,256]{2,1,0:T(8,128)(2,1)}), bf16[8,144,256]{2,1,0:T(8,128)(2,1)S(1)}, u32[]{:S(2)}, u32[]{:S(2)}) %all-to-all-start.4) | async-done | bytes 589856 | tf_op jit(solution)/shard_map/all_to_all | solution.py:643
  187.2 1.8 last.1
  189.0 4.3 %all-to-all-start.5 = ((bf16[8,64,256]{2,1,0:T(8,128)(2,1)}), bf16[8,64,256]{2,1,0:T(8,128)(2,1)S(1)}, u32[]{:S(2)}, u32[]{:S(2)}) async-start(bf16[8,64,256]{2,1,0:T(8,128)(2,1)} %last.1), calls=%async_computation.5 | async-start | bytes 524288 | tf_op jit(solution)/shard_map/all_to_all | solution.py:652
  193.3 1.7 slice.18
  196.4 3.3 %all-to-all-done.5 = bf16[8,64,256]{2,1,0:T(8,128)(2,1)S(1)} async-done(((bf16[8,64,256]{2,1,0:T(8,128)(2,1)}), bf16[8,64,256]{2,1,0:T(8,128)(2,1)S(1)}, u32[]{:S(2)}, u32[]{:S(2)}) %all-to-all-start.5) | async-done | bytes 262176 | tf_op jit(solution)/shard_map/all_to_all | solution.py:652
  (28 shorter events, 9.1 us)
Async XLA Ops:
  2.9 15.0 %all-to-all-start = ((s32[16,1,1]{2,1,0:T(1,128)}), s32[16,1,1]{2,1,0:T(1,128)S(1)}, u32[]{:S(2)}, u32[]{:S(2)}) async-start(s32[16,1,1]{2,1,0:T(1,128)} %copy.52), calls=%async_computation | async-start | bytes 16384 | tf_op jit(solution)/shard_map/all_to_all | solution.py:454
  18.5 2.7 %copy-start.3 = (s32[16]{0:T(128)}, s32[16]{0:T(128)S(1)}, u32[]{:S(2)}) copy-start(s32[16]{0:T(128)S(1)} %get-tuple-element.43.requested) | copy-start | bytes 196
  21.3 18.6 %all-to-all-start.1 = ((bf16[16,128,256]{2,1,0:T(8,128)(2,1)}), bf16[16,128,256]{2,1,0:T(8,128)(2,1)S(1)}, u32[]{:S(2)}, u32[]{:S(2)}) async-start(bf16[16,128,256]{2,1,0:T(8,128)(2,1)} %broadcast_select_fusion), calls=%async_computation.1 | async-start | bytes 2097152 | tf_op jit(solution)/shard_map/all_to_all | solution.py:468
  39.8 1.0 copy-start
  103.9 32.9 %all-to-all-start.2 = ((bf16[8,88,256]{2,1,0:T(8,128)(2,1)}), bf16[8,88,256]{2,1,0:T(8,128)(2,1)S(1)}, u32[]{:S(2)}, u32[]{:S(2)}) async-start(bf16[8,88,256]{2,1,0:T(8,128)(2,1)} %get-tuple-element.36), calls=%async_computation.2 | async-start | bytes 720896 | tf_op jit(solution)/shard_map/all_to_all | solution.py:569
  136.9 0.7 copy-start.2
  170.4 15.9 %all-to-all-start.4 = ((bf16[8,144,256]{2,1,0:T(8,128)(2,1)}), bf16[8,144,256]{2,1,0:T(8,128)(2,1)S(1)}, u32[]{:S(2)}, u32[]{:S(2)}) async-start(bf16[8,144,256]{2,1,0:T(8,128)(2,1)} %get-tuple-element.40), calls=%async_computation.4 | async-start | bytes 1179648 | tf_op jit(solution)/shard_map/all_to_all | solution.py:643
  186.4 0.8 copy-start.1
  189.0 10.8 %all-to-all-start.5 = ((bf16[8,64,256]{2,1,0:T(8,128)(2,1)}), bf16[8,64,256]{2,1,0:T(8,128)(2,1)S(1)}, u32[]{:S(2)}, u32[]{:S(2)}) async-start(bf16[8,64,256]{2,1,0:T(8,128)(2,1)} %last.1), calls=%async_computation.5 | async-start | bytes 524288 | tf_op jit(solution)/shard_map/all_to_all | solution.py:652

commit v3 on v2

--- a/solution.py
+++ b/solution.py
@@ -9,6 +9,7 @@
 
 NEG_LARGE = -1e30
 GROUP = 8
+FIRST_GROUP = 8
 F32 = jnp.float32
 BF16 = jnp.bfloat16
 VMEM_LIMIT = 60 * 1024 * 1024
@@ -32,6 +33,20 @@
 
 def only_head(x, head_of_lane, head):
     return jnp.where(head_of_lane == head, x, jnp.zeros_like(x))
+
+
+def fill_bases(base_s, frames_here, first_row, frames_send, right, edge_gain):
+    block, edge_width = right.shape
+    frame_rows = jnp.broadcast_to(frames_send[...].astype(F32), (block, edge_width)).T.astype(jnp.int32)
+    same = right + edge_gain[...].astype(F32) * 0.5
+    first_frame = frames_here[first_row]
+
+    def fill(at, carry):
+        base_s[pl.ds(pl.multiple_of(at * block, block), block), :] = jnp.where(frame_rows == first_frame + at, same, right)
+        return carry
+
+    lax.fori_loop(0, frames_here[first_row + block - 1] - first_frame + 1, fill, 0)
+    return first_frame
 
 
 def first_kernel(
@@ -39,7 +54,7 @@
     own, local, got, d_out, frames_send, mask,
     w_query, w_key, w_value, w_left, w_right, w_edge_value, w_out, edge_gain, w_bias,
     probs_out, pair_out, ctx_out, stats_out, att_out, query_out, keys_out, datt_out, left_out, right_out,
-    qk_s, dp_s, pair_s, edge_s, score_s,
+    qk_s, dp_s, dctx_s, query_s, datt_s, stack_s, edge_s, score_s, base_s,
 ):
     slot = pl.program_id(0)
     block, att_width = query_out.shape
@@ -65,44 +80,50 @@
         send_x = jnp.where(table[slot, IS_LOCAL] > 0, local[...].astype(F32), got[...].astype(F32)).astype(BF16)
         query = dot(own_x, w_query[...]).astype(BF16)
         keys = dot(send_x, w_key[...]).astype(BF16)
-        values = dot(send_x, w_value[...]).astype(BF16)
-        left = dot(own_x, w_left[...]).astype(BF16).astype(F32) * 0.5
+        left_out[...] = dot(own_x, w_left[...]).astype(BF16).astype(F32) * 0.5
         right = dot(send_x, w_right[...]).astype(BF16).astype(F32) * 0.5
         d_att = dot_t(d_out[...], w_out[...]).astype(BF16)
         query_out[...] = query
         keys_out[...] = keys
         datt_out[...] = d_att
-        left_out[...] = left
         right_out[...] = right
-        frame_rows = jnp.broadcast_to(frames_send[...].astype(F32), (block, edge_width)).T.astype(jnp.int32)
-        right_same = right + edge_gain[...].astype(F32) * 0.5
-        head_of_lane = head_lanes(heads, att_width, block)
-        bias_row = w_bias[...].astype(F32)
-        values_edge = jnp.concatenate([values, w_edge_value[...]], axis=0)
-        for h in range(heads):
-            qk_s[pl.ds(h, block, stride=heads), :] = dot_t(only_head(query, head_of_lane, h), keys) * scale
-            both = dot_t(only_head(d_att, head_of_lane, h), values_edge)
-            dp_s[pl.ds(h, block, stride=heads), :] = both[:, :block]
-            pair_s[pl.ds(heads + h, block, stride=2 * heads), :] = both[:, block:]
-            pair_s[pl.ds(h, block, stride=2 * heads), :] = jnp.broadcast_to(bias_row[h : h + 1], (block, edge_width))
+        query_s[...] = query.astype(F32)
+        datt_s[...] = d_att.astype(F32)
+        stack_s[:block, :] = dot(send_x, w_value[...]).astype(BF16)
+        stack_s[block:, :] = w_edge_value[...]
+        first_row = table[slot, RECV_BLOCK] * block
+        first_frame = fill_bases(base_s, frames_here, first_row, frames_send, right, edge_gain)
+        own_head = head_lanes(heads, att_width, heads) == lax.broadcasted_iota(jnp.int32, (heads, att_width), 0)
+        bias_rows = w_bias[...].astype(F32)
         valid = jnp.broadcast_to(mask[...], (heads, block)) > 0
         lane = lax.broadcasted_iota(jnp.int32, (heads, block), 1)
-        first_row = table[slot, RECV_BLOCK] * block
-
-        groups = block // GROUP
+        groups = block // FIRST_GROUP
+
+        def by_head(rows_ref, at):
+            rows = [
+                jnp.where(own_head, jnp.broadcast_to(rows_ref[pl.ds(at * FIRST_GROUP + k, 1), :], own_head.shape), 0.0)
+                for k in range(FIRST_GROUP)
+            ]
+            return jnp.concatenate(rows, axis=0).astype(BF16)
 
         def edge_stage(at):
-            for k in range(GROUP):
-                i = at * GROUP + k
-                half = jnp.where(frame_rows == frames_here[first_row + i], right_same, right)
-                half = half + left_out[pl.ds(i, 1), :]
+            rows = pl.ds(pl.multiple_of(at * FIRST_GROUP * heads, FIRST_GROUP * heads), FIRST_GROUP * heads)
+            qk_s[rows, :] = dot_t(by_head(query_s, at), keys_out[...]) * scale
+            both = dot_t(by_head(datt_s, at), stack_s[...])
+            dp_s[rows, :] = both[:, :block]
+            dctx_s[rows, :] = both[:, block:]
+            for k in range(FIRST_GROUP):
+                i = at * FIRST_GROUP + k
+                base_row = pl.multiple_of((frames_here[first_row + i] - first_frame) * block, block)
+                half = base_s[pl.ds(base_row, block), :] + left_out[pl.ds(i, 1), :]
                 edge_s[pl.ds(pl.multiple_of(i * block, block), block), :] = (half * jnp.tanh(half) + half).astype(BF16)
 
         def score_stage(at):
-            for pair in range(GROUP // 2):
-                i = at * GROUP + 2 * pair
+            for pair in range(FIRST_GROUP // 2):
+                i = at * FIRST_GROUP + 2 * pair
                 rows = pl.ds(pl.multiple_of(i * both_heads, 2 * both_heads), 2 * both_heads)
-                pair_rows = pair_s[rows, :].astype(BF16)
+                d_ctx = dctx_s[pl.ds(pl.multiple_of(i * heads, both_heads), both_heads), :]
+                pair_rows = jnp.concatenate([bias_rows, d_ctx[:heads], bias_rows, d_ctx[heads:]], axis=0).astype(BF16)
                 pair_out[rows, :] = pair_rows
                 scores = dot_t(pair_rows, edge_s[pl.ds(pl.multiple_of(i * block, 2 * block), 2 * block), :])
                 for k in range(2):
@@ -113,8 +134,8 @@
 
         def soft_stage(at, carry):
             tops, totals, deltas = carry
-            for k in range(GROUP):
-                i = at * GROUP + k
+            for k in range(FIRST_GROUP):
+                i = at * FIRST_GROUP + k
                 row = pl.multiple_of(i * heads, heads)
                 both_row = pl.multiple_of(i * both_heads, both_heads)
                 logits = qk_s[pl.ds(row, heads), :] + score_s[pl.ds(both_row, heads), :]
@@ -123,8 +144,10 @@
                 top = jnp.max(logits, axis=1, keepdims=True)
                 probs = jnp.exp(logits - top)
                 total = jnp.sum(probs, axis=1, keepdims=True)
-                probs = probs * (1.0 / total)
                 delta = jnp.sum(probs * d_prob, axis=1, keepdims=True)
+                inverse = 1.0 / total
+                probs = probs * inverse
+                delta = delta * inverse
                 probs_out[pl.ds(both_row, heads), :] = probs
                 probs_out[pl.ds(both_row + heads, heads), :] = probs * (d_prob - delta)
                 here = lane == i
@@ -134,8 +157,8 @@
             return tops, totals, deltas
 
         def ctx_stage(at):
-            for pair in range(GROUP // 2):
-                i = at * GROUP + 2 * pair
+            for pair in range(FIRST_GROUP // 2):
+                i = at * FIRST_GROUP + 2 * pair
                 rows = pl.ds(pl.multiple_of(i * both_heads, 2 * both_heads), 2 * both_heads)
                 edges = edge_s[pl.ds(pl.multiple_of(i * block, 2 * block), 2 * block), :]
                 sums = dot(probs_out[rows, :].astype(BF16), jnp.concatenate([edges[:block], edges[block:]], axis=1))
@@ -160,12 +183,12 @@
         stats_out[TOP] = tops
         stats_out[TOTAL] = totals
         stats_out[DELTA] = deltas
+        head_of_lane = head_lanes(heads, att_width, block)
         att = jnp.zeros((block, att_width), F32)
         for h in range(heads):
-            probs_h = probs_out[pl.ds(h, block, stride=2 * heads), :].astype(BF16)
-            ctx_h = ctx_out[pl.ds(h, block, stride=2 * heads), :].astype(BF16)
-            att += dot(probs_h, only_head(values, head_of_lane, h))
-            att += dot(ctx_h, only_head(w_edge_value[...], head_of_lane, h))
+            rows = pl.ds(h, block, stride=both_heads)
+            lhs = jnp.concatenate([probs_out[rows, :], ctx_out[rows, :]], axis=1).astype(BF16)
+            att = jnp.where(head_of_lane == h, dot(lhs, stack_s[...]), att)
         att_out[...] = att
 
 
@@ -217,18 +240,20 @@
         )
         first_row = pl.multiple_of(table[slot, RECV_BLOCK] * block, block)
         att_s[pl.ds(first_row, block), :] += att[...] * share_rows
-        scaled = (d_att[...].astype(F32) * share_rows).astype(BF16)
+        scaled = d_att[...].astype(F32) * share_rows
         weights = jnp.concatenate([share, share * shift], axis=0).astype(BF16)
-        head_of_lane = head_lanes(heads, att_width, block)
         head_of_row = lax.broadcasted_iota(jnp.int32, (heads, edge_width), 0)
-        edge = jnp.zeros((edge_width, att_width), F32)
+        head_dim = att_width // heads
+        scaled_t = scaled.T.astype(BF16)
+        edge = []
         bias = jnp.zeros((heads, edge_width), F32)
         for h in range(heads):
-            ctx_h = ctx[pl.ds(h, block, stride=2 * heads), :]
+            ctx_h = ctx[pl.ds(h, block, stride=2 * heads), :].astype(BF16)
             moved_h = ctx[pl.ds(heads + h, block, stride=2 * heads), :].astype(BF16)
-            edge += dot(ctx_h.T.astype(BF16), only_head(scaled, head_of_lane, h))
-            sums = dot(weights, jnp.concatenate([ctx_h.astype(BF16), moved_h], axis=1))
+            edge.append(dot(scaled_t[h * head_dim : (h + 1) * head_dim], ctx_h))
+            sums = dot(weights, jnp.concatenate([ctx_h, moved_h], axis=1))
             bias += jnp.where(head_of_row == h, sums[:heads, edge_width:] + sums[heads:, :edge_width], 0.0)
+        edge = jnp.concatenate(edge, axis=0)
         edge_s[...] += edge
         bias_s[...] += bias
 
@@ -237,9 +262,10 @@
         n_send = message.shape[0]
         rows = att_s.shape[0] // n_send
         edge_rows = edge_width // n_send
+        edge_all = edge_s[...].T
         for s in range(n_send):
             message[s, 0:rows, :] = att_s[s * rows : (s + 1) * rows, :].astype(BF16)
-            message[s, rows : rows + edge_rows, :] = edge_s[s * edge_rows : (s + 1) * edge_rows, :].astype(BF16)
+            message[s, rows : rows + edge_rows, :] = edge_all[s * edge_rows : (s + 1) * edge_rows, :].astype(BF16)
             message[s, rows + edge_rows :, :] = jnp.concatenate([bias_s[...]] * (att_width // edge_width), axis=1).astype(BF16)
 
 
@@ -248,7 +274,7 @@
     share_in, shift_in, probs_in, pair_in, query_in, keys_in, datt_in, left_in, right_in, frames_send,
     w_query, w_key, w_value, w_left, w_right, edge_gain,
     recv_out, send_out,
-    rows_s, diag_s, d_edge_s, right_s, same_s, frame_s, grad_right_s, grad_left_s,
+    rows_s, diag_s, even_s, odd_s, base_s, grad_right_s, grad_left_s,
 ):
     slot = pl.program_id(0)
     block, att_width = query_in.shape
@@ -271,14 +297,16 @@
     @pl.when(live)
     def _():
         share, shift = share_in[...], shift_in[...]
-        right_s[...] = right_in[...]
-        same_s[...] = right_in[...] + edge_gain[...].astype(F32) * 0.5
-        frame_s[...] = jnp.broadcast_to(frames_send[...].astype(F32), (block, edge_width)).T.astype(jnp.int32)
+        first_row = table[slot, RECV_BLOCK] * block
+        first_frame = fill_bases(base_s, frames_here, first_row, frames_send, right_in[...], edge_gain)
         grad_right_s[...] = jnp.zeros_like(grad_right_s)
+        even_s[...] = jnp.zeros_like(even_s)
+        odd_s[...] = jnp.zeros_like(odd_s)
+        rows_s[: GROUP * both_heads, :] = jnp.zeros((GROUP * both_heads, block), F32)
         lane = lax.broadcasted_iota(jnp.int32, (heads, block), 1)
-        first_row = table[slot, RECV_BLOCK] * block
-
-        def group(at, carry):
+        groups = block // GROUP
+
+        def row_stage(at):
             for k in range(GROUP):
                 i = at * GROUP + k
                 here = lane == i
@@ -289,23 +317,32 @@
                 centred = probs_in[pl.ds(row + heads, heads), :]
                 rows_s[pl.ds(row, heads), :] = (centred + moved * probs) * factor
                 rows_s[pl.ds(row + heads, heads), :] = probs * factor
+
+        def edge_stage(at, d_edge_s):
+            first = pl.multiple_of(at * GROUP * both_heads, GROUP * both_heads)
+            across = rows_s[pl.ds(first, GROUP * both_heads), :].T.astype(BF16)
+            for k in range(GROUP):
+                row = pl.multiple_of((at * GROUP + k) * both_heads, both_heads)
                 diag_s[both_heads * k : both_heads * (k + 1), edge_width * k : edge_width * (k + 1)] = (
                     pair_in[pl.ds(row, both_heads), :]
                 )
-            first = pl.multiple_of(at * GROUP * both_heads, GROUP * both_heads)
-            across = rows_s[pl.ds(first, GROUP * both_heads), :].T.astype(BF16)
-            d_edge_s[...] = dot(across, diag_s[...])
-            frame_of = [frames_here[first_row + at * GROUP + k] for k in range(GROUP)]
+            for col in range(0, GROUP * edge_width, 2 * edge_width):
+                d_edge_s[:, col : col + 2 * edge_width] = dot(across, diag_s[:, col : col + 2 * edge_width])
+
+        def slope_stage(at, d_edge_s):
+            base_of = [
+                pl.multiple_of((frames_here[first_row + at * GROUP + k] - first_frame) * block, block)
+                for k in range(GROUP)
+            ]
             left_of = [
                 jnp.broadcast_to(left_in[pl.ds(at * GROUP + k, 1), :], (8, edge_width)) for k in range(GROUP)
             ]
             left_sums = [jnp.zeros((8, edge_width), F32) for _ in range(GROUP)]
             for tile in range(tiles):
                 span = slice(8 * tile, 8 * tile + 8)
-                right_t, same_t, frame_t = right_s[span, :], same_s[span, :], frame_s[span, :]
                 right_sum = grad_right_s[span, :]
                 for k in range(GROUP):
-                    half = jnp.where(frame_t == frame_of[k], same_t, right_t) + left_of[k]
+                    half = base_s[pl.ds(base_of[k] + 8 * tile, 8), :] + left_of[k]
                     tanh = jnp.tanh(half)
                     slope = (1.0 + tanh) * (half - half * tanh + 1.0)
                     d_pre = slope * d_edge_s[span, edge_width * k : edge_width * (k + 1)]
@@ -314,20 +351,30 @@
                 grad_right_s[span, :] = right_sum
             for k in range(GROUP):
                 grad_left_s[pl.ds(at * GROUP + k, 1), :] = jnp.sum(left_sums[k], axis=0, keepdims=True)
+
+        buffers = (even_s, odd_s)
+
+        def step(two, carry):
+            for parity in range(2):
+                at = 2 * two + parity
+                slope_stage(jnp.clip(at - 2, 0, groups - 1), buffers[parity])
+                edge_stage(jnp.clip(at - 1, 0, groups - 1), buffers[1 - parity])
+                row_stage(jnp.clip(at, 0, groups - 1))
             return carry
 
-        lax.fori_loop(0, block // GROUP, group, 0)
+        lax.fori_loop(0, (groups + 2) // 2, step, 0)
         query, keys, d_att = query_in[...], keys_in[...], datt_in[...]
         head_of_lane = head_lanes(heads, att_width, block)
         grad_query = jnp.zeros((block, att_width), F32)
         grad_keys = jnp.zeros((block, att_width), F32)
         grad_values = jnp.zeros((block, att_width), F32)
         for h in range(heads):
-            d_logit = rows_s[pl.ds(h, block, stride=both_heads), :]
-            weight = rows_s[pl.ds(heads + h, block, stride=both_heads), :]
-            grad_query += dot(d_logit.astype(BF16), only_head(keys, head_of_lane, h))
-            grad_keys += dot(d_logit.T.astype(BF16), only_head(query, head_of_lane, h))
-            grad_values += dot(weight.T.astype(BF16), only_head(d_att, head_of_lane, h))
+            this = head_of_lane == h
+            d_logit = rows_s[pl.ds(h, block, stride=both_heads), :].astype(BF16)
+            weight = rows_s[pl.ds(heads + h, block, stride=both_heads), :].astype(BF16)
+            grad_query = jnp.where(this, dot(d_logit, keys), grad_query)
+            grad_keys = jnp.where(this, dot(d_logit.T, query), grad_keys)
+            grad_values = jnp.where(this, dot(weight.T, d_att), grad_values)
         recv_out[...] = dot_t((grad_query * scale).astype(BF16), w_query[...]) + dot_t(
             (grad_left_s[...] * 0.5).astype(BF16), w_left[...]
         )
@@ -520,9 +567,13 @@
             scratch_shapes=[
                 pltpu.VMEM((block * heads, block), F32),
                 pltpu.VMEM((block * heads, block), F32),
-                pltpu.VMEM((block * both, edge_width), F32),
+                pltpu.VMEM((block * heads, edge_width), F32),
+                pltpu.VMEM((block, att_width), F32),
+                pltpu.VMEM((block, att_width), F32),
+                pltpu.VMEM((2 * block, att_width), BF16),
                 pltpu.VMEM((block * block, edge_width), BF16),
                 pltpu.VMEM((block * both, block), F32),
+                pltpu.VMEM((block * block, edge_width), F32),
             ],
         ),
         compiler_params=params(),
@@ -559,7 +610,7 @@
             ],
             scratch_shapes=[
                 pltpu.VMEM((rows, att_width), F32),
-                pltpu.VMEM((edge_width, att_width), F32),
+                pltpu.VMEM((att_width, edge_width), F32),
                 pltpu.VMEM((heads, edge_width), F32),
             ],
         ),
@@ -597,9 +648,8 @@
                 pltpu.VMEM((block * both, block), F32),
                 pltpu.VMEM((GROUP * both, GROUP * edge_width), BF16),
                 pltpu.VMEM((block, GROUP * edge_width), F32),
-                pltpu.VMEM((block, edge_width), F32),
-                pltpu.VMEM((block, edge_width), F32),
-                pltpu.VMEM((block, edge_width), jnp.int32),
+                pltpu.VMEM((block, GROUP * edge_width), F32),
+                pltpu.VMEM((block * block, edge_width), F32),
                 pltpu.VMEM((block, edge_width), F32),
                 pltpu.VMEM((block, edge_width), F32),
             ],

time: 202 us -> 187 us (0.926)
  blocking collectives: 52.2 us -> 40.4 us
    all_gather x1, blocking collectives: 24.6 us -> 17.4 us  [body(): stats_all = lax.all_gather(stats, 'send', axis=0, tiled=True)]
    all_to_all x1, blocking collectives: 27.6 us -> 23 us  [body(): lax.all_to_all(message, 'recv', split_axis=0, concat_axis=0, tiled=True)]
    pallas_call x1, Pallas kernels: 29.3 us -> 27.2 us  [body(): pl.pallas_call(grad_kernel, out_shape=(shape_of(F32, block, att_width), s...]
where the time goes in v3:
time: 187 us; the launch traced here: 186 us
  Pallas kernels  73.4 us (39%)
  blocking collectives  40.4 us (22%)
  waiting for transfers between devices  28.2 us (15%)
  starting transfers between devices  25 us (13%)
  local copies, waits for them, and re-layouts  12.3 us (7%)
  other arithmetic  6.26 us (3%)
    pallas_call x1, Pallas kernels, body(): pl.pallas_call(first_kernel, out_shape=tuple((shape_of(*o) for o in outs)...  31.8 us
    pallas_call x1, Pallas kernels, body(): pl.pallas_call(grad_kernel, out_shape=(shape_of(F32, block, att_width), s...  27.2 us
    all_to_all x1, blocking collectives, body(): lax.all_to_all(message, 'recv', split_axis=0, concat_axis=0, tiled=True)  23 us
    all_gather x1, blocking collectives, body(): stats_all = lax.all_gather(stats, 'send', axis=0, tiled=True)  17.4 us
    all_to_all x1, waiting for transfers between devices, body(): lax.all_to_all(replies, 'recv', split_axis=0, concat_axis=0, tiled=True)  10.8 us
    all_to_all x1, waiting for transfers between devices, body(): lax.all_to_all(message, 'send', split_axis=0, concat_axis=0, tiled=True)  8.68 us
    all_to_all x1, starting transfers between devices, body(): lax.all_to_all(wanted, 'recv', split_axis=0, concat_axis=0, tiled=True)  8.59 us
    pallas_call x1, Pallas kernels, body(): pl.pallas_call(mid_kernel, out_shape=(shape_of(F32, heads, block), shape_...  7.46 us
  transfers between devices with their start and end apart: 5, of which 4 were waited for; matrix products, arithmetic and copies ran while one was open for 5% of the time, Pallas kernels for 15%

profile of v3, /device:TPU:1, one launch (start us, length us, event | category | flops | bytes accessed | tf_op | source)
XLA Modules:
  0.0 186.4 jit_solution(10170052702944678036)
XLA Ops:
  2.9 8.6 %all-to-all-start = ((s32[16,1,1]{2,1,0:T(1,128)}), s32[16,1,1]{2,1,0:T(1,128)S(1)}, u32[]{:S(2)}, u32[]{:S(2)}) async-start(s32[16,1,1]{2,1,0:T(1,128)} %copy.52), calls=%async_computation | async-start | bytes 16384 | tf_op jit(solution)/shard_map/all_to_all | solution.py:501
  12.5 5.4 %all-to-all-done = s32[16,1,1]{2,1,0:T(1,128)S(1)} async-done(((s32[16,1,1]{2,1,0:T(1,128)}), s32[16,1,1]{2,1,0:T(1,128)S(1)}, u32[]{:S(2)}, u32[]{:S(2)}) %all-to-all-start) | async-done | bytes 96 | tf_op jit(solution)/shard_map/all_to_all | solution.py:501
  18.5 1.6 gather_fusion
  20.1 1.1 broadcast_select_fusion
  21.3 3.7 %all-to-all-start.1 = ((bf16[16,128,256]{2,1,0:T(8,128)(2,1)}), bf16[16,128,256]{2,1,0:T(8,128)(2,1)S(1)}, u32[]{:S(2)}, u32[]{:S(2)}) async-start(bf16[16,128,256]{2,1,0:T(8,128)(2,1)} %broadcast_select_fusion), calls=%async_computation.1 | async-start | bytes 2097152 | tf_op jit(solution)/shard_map/all_to_all | solution.py:515
  25.0 1.3 dynamic_slice.9.frames_here
  27.1 1.4 constant_dynamic-slice_fusion.1.nodes_piece
  29.0 10.8 %all-to-all-done.1.got = bf16[16,128,256]{2,1,0:T(8,128)(2,1)S(1)} async-done(((bf16[16,128,256]{2,1,0:T(8,128)(2,1)}), bf16[16,128,256]{2,1,0:T(8,128)(2,1)S(1)}, u32[]{:S(2)}, u32[]{:S(2)}) %all-to-all-start.1) | async-done | bytes 1048608 | tf_op jit(solution)/shard_map/all_to_all | solution.py:515
  39.8 1.0 copy-done
  40.8 31.8 %first.1 = (f32[4,2048,128]{2,1,0:T(8,128)}, bf16[4,2048,128]{2,1,0:T(8,128)(2,1)}, f32[4,2048,128]{2,1,0:T(8,128)}, f32[4,4,8,128]{3,2,1,0:T(8,128)}, f32[4,128...) custom-call(s32[4,6]{1,0:T(4,128)} %stack.2.table, ...), custom_call_target="tpu_custom_call" | custom-call | tf_op jit(solution)/shard_map/first/pallas_call | solution.py:543
  72.6 17.4 %all_gather.3.stats_all = f32[32,4,8,128]{3,2,1,0:T(8,128)} all-gather(f32[4,4,8,128]{3,2,1,0:T(8,128)} %get-tuple-element.23.stats_mine), channel_id=1, replica_groups=mesh['recv'=16,'send'=8] {'send'}, dimensions={0}, use_global_device_ids=true | all-gather | bytes 589824 | tf_op jit(solution)/shard_map/all_gather | solution.py:587
  90.0 7.5 %mid.1 = (f32[4,8,128]{2,1,0:T(8,128)}, f32[4,8,128]{2,1,0:T(8,128)}, bf16[8,88,256]{2,1,0:T(8,128)(2,1)}) custom-call(s32[4,6]{1,0:T(4,128)} %stack.2.table, f32[32,4,8,128]{3,2,1,0:T(8,128)} %all_gather.3.stats_all, f32[4,4,8,128]{3,2,1,0:T(8,128)} %get-tuple-element.23.stats_mine, f32[4,2048,128]{2,1,0:T(8,128)} %get-tuple-element.24.ctx, ...), custom_call_target="tpu_custom_call" | custom-call | tf_op jit(solution)/shard_map/mid/pallas_call | solution.py:589
  97.4 3.5 %all-to-all-start.2 = ((bf16[8,88,256]{2,1,0:T(8,128)(2,1)}), bf16[8,88,256]{2,1,0:T(8,128)(2,1)S(1)}, u32[]{:S(2)}, u32[]{:S(2)}) async-start(bf16[8,88,256]{2,1,0:T(8,128)(2,1)} %get-tuple-element.36), calls=%async_computation.2 | async-start | bytes 720896 | tf_op jit(solution)/shard_map/all_to_all | solution.py:620
  100.9 27.2 %grad.1 = (f32[4,128,256]{2,1,0:T(8,128)}, bf16[4,128,256]{2,1,0:T(8,128)(2,1)}) custom-call(s32[4,6]{1,0:T(4,128)} %stack.2.table, s32[512]{0:T(512)} %dynamic_slice.9.frames_here, f32[4,8,128]{2,1,0:T(8,128)} %get-tuple-element.27.share_in, f32[4,8,128]{2,1,0:T(8,128)} %get-tuple-element.28.shift_in, f32[4,2048,128]{2,1,0:T(8,128)} %get-tuple-element.29.probs_in, ...), custom_call_target="tpu_custom_call" | custom-call | flops 40000000000 | bytes 12000000 | tf_op jit(solution)/shard_map/grad/pallas_call | solution.py:622
  128.9 2.5 %pack.1 = (bf16[16,152,256]{2,1,0:T(8,128)(2,1)}, bf16[64,256]{1,0:T(8,128)(2,1)}) custom-call(s32[16]{0:T(128)} %broadcast_add_fusion.slot_of_owner, bf16[4,128,256]{2,1,0:T(8,128)(2,1)} %get-tuple-element.35.send_part, bf16[8,88,256]{2,1,0:T(8,128)(2,1)} %copy-done.2, bf16[64,256]{1,0:T(8,128)(2,1)} %constant_dynamic-slice_fusion.1.nodes_piece, ...), custom_call_target="tpu_custom_call" | custom-call | tf_op jit(solution)/shard_map/pack/pallas_call | solution.py:669
  131.5 23.0 %all_to_all.36.back = bf16[16,152,256]{2,1,0:T(8,128)(2,1)} all-to-all(bf16[16,152,256]{2,1,0:T(8,128)(2,1)} %get-tuple-element.37), channel_id=1, replica_groups=mesh['recv'=16,'send'=8] {'recv'}, dimensions={0} | all-to-all | bytes 2490368 | tf_op jit(solution)/shard_map/all_to_all | solution.py:680
  154.5 2.6 %merge.1 = (bf16[8,144,256]{2,1,0:T(8,128)(2,1)}, f32[8,128]{1,0:T(8,128)}) custom-call(s32[4,6]{1,0:T(4,128)} %stack.2.table, s32[16]{0:T(128)} %copy-done.3, bf16[16,152,256]{2,1,0:T(8,128)(2,1)} %all_to_all.36.back, f32[4,128,256]{2,1,0:T(8,128)} %get-tuple-element.38.recv_part, bf16[4,128,256]{2,1,0:T(8,128)(2,1)} %get-tuple-element.35.send_part, ...), custom_call_target="tpu_custom_call" | custom-call | tf_op jit(solution)/shard_map/merge/pallas_call | solution.py:681
  157.1 5.0 %all-to-all-start.4 = ((bf16[8,144,256]{2,1,0:T(8,128)(2,1)}), bf16[8,144,256]{2,1,0:T(8,128)(2,1)S(1)}, u32[]{:S(2)}, u32[]{:S(2)}) async-start(bf16[8,144,256]{2,1,0:T(8,128)(2,1)} %get-tuple-element.40), calls=%async_computation.4 | async-start | bytes 1179648 | tf_op jit(solution)/shard_map/all_to_all | solution.py:693
  162.1 1.4 constant_dynamic-slice_fusion.d_out_piece
  163.4 8.7 %all-to-all-done.4.parts = bf16[8,144,256]{2,1,0:T(8,128)(2,1)S(1)} async-done(((bf16[8,144,256]{2,1,0:T(8,128)(2,1)}), bf16[8,144,256]{2,1,0:T(8,128)(2,1)S(1)}, u32[]{:S(2)}, u32[]{:S(2)}) %all-to-all-start.4) | async-done | bytes 589856 | tf_op jit(solution)/shard_map/all_to_all | solution.py:693
  172.9 1.8 last.1
  174.7 4.3 %all-to-all-start.5 = ((bf16[8,64,256]{2,1,0:T(8,128)(2,1)}), bf16[8,64,256]{2,1,0:T(8,128)(2,1)S(1)}, u32[]{:S(2)}, u32[]{:S(2)}) async-start(bf16[8,64,256]{2,1,0:T(8,128)(2,1)} %last.1), calls=%async_computation.5 | async-start | bytes 524288 | tf_op jit(solution)/shard_map/all_to_all | solution.py:702
  179.0 1.7 slice.18
  182.2 3.3 %all-to-all-done.5 = bf16[8,64,256]{2,1,0:T(8,128)(2,1)S(1)} async-done(((bf16[8,64,256]{2,1,0:T(8,128)(2,1)}), bf16[8,64,256]{2,1,0:T(8,128)(2,1)S(1)}, u32[]{:S(2)}, u32[]{:S(2)}) %all-to-all-start.5) | async-done | bytes 262176 | tf_op jit(solution)/shard_map/all_to_all | solution.py:702
  (28 shorter events, 9.1 us)
Async XLA Ops:
  2.9 15.0 %all-to-all-start = ((s32[16,1,1]{2,1,0:T(1,128)}), s32[16,1,1]{2,1,0:T(1,128)S(1)}, u32[]{:S(2)}, u32[]{:S(2)}) async-start(s32[16,1,1]{2,1,0:T(1,128)} %copy.52), calls=%async_computation | async-start | bytes 16384 | tf_op jit(solution)/shard_map/all_to_all | solution.py:501
  18.5 2.7 %copy-start.3 = (s32[16]{0:T(128)}, s32[16]{0:T(128)S(1)}, u32[]{:S(2)}) copy-start(s32[16]{0:T(128)S(1)} %get-tuple-element.43.requested) | copy-start | bytes 196
  21.3 18.6 %all-to-all-start.1 = ((bf16[16,128,256]{2,1,0:T(8,128)(2,1)}), bf16[16,128,256]{2,1,0:T(8,128)(2,1)S(1)}, u32[]{:S(2)}, u32[]{:S(2)}) async-start(bf16[16,128,256]{2,1,0:T(8,128)(2,1)} %broadcast_select_fusion), calls=%async_computation.1 | async-start | bytes 2097152 | tf_op jit(solution)/shard_map/all_to_all | solution.py:515
  39.8 1.0 copy-start
  97.4 30.8 %all-to-all-start.2 = ((bf16[8,88,256]{2,1,0:T(8,128)(2,1)}), bf16[8,88,256]{2,1,0:T(8,128)(2,1)S(1)}, u32[]{:S(2)}, u32[]{:S(2)}) async-start(bf16[8,88,256]{2,1,0:T(8,128)(2,1)} %get-tuple-element.36), calls=%async_computation.2 | async-start | bytes 720896 | tf_op jit(solution)/shard_map/all_to_all | solution.py:620
  128.2 0.7 copy-start.2
  157.1 15.0 %all-to-all-start.4 = ((bf16[8,144,256]{2,1,0:T(8,128)(2,1)}), bf16[8,144,256]{2,1,0:T(8,128)(2,1)S(1)}, u32[]{:S(2)}, u32[]{:S(2)}) async-start(bf16[8,144,256]{2,1,0:T(8,128)(2,1)} %get-tuple-element.40), calls=%async_computation.4 | async-start | bytes 1179648 | tf_op jit(solution)/shard_map/all_to_all | solution.py:693
  172.1 0.8 copy-start.1
  174.7 10.8 %all-to-all-start.5 = ((bf16[8,64,256]{2,1,0:T(8,128)(2,1)}), bf16[8,64,256]{2,1,0:T(8,128)(2,1)S(1)}, u32[]{:S(2)}, u32[]{:S(2)}) async-start(bf16[8,64,256]{2,1,0:T(8,128)(2,1)} %last.1), calls=%async_computation.5 | async-start | bytes 524288 | tf_op jit(solution)/shard_map/all_to_all | solution.py:702
